TPU v7x, 32 devices: a whole 2x2x4 slice. The times are simulated.
32 devices in a mesh: bra: 4 (over z), ket: 2 (over y), pair: 4 (over x, core).
Axes of the slice: x: 2, y: 2, z: 4, core: 2. Of those that a mesh axis runs over, the one named last changes fastest.
Arguments:
- amplitudes: bfloat16 [1536, 8, 1536], P('pair', ('bra', 'ket')), may hold values from -6 to 6
- integrals: bfloat16 [8, 4, 128, 1536], P(('bra', 'ket'), 'pair'), may hold values from -0.25 to 0.25
- screen_list: int32 [8, 4], P(('bra', 'ket')), may hold values from 0 to 11
- block_owner: int32 [8, 4], P(('bra', 'ket')), may hold values from 0 to 7, all different within a row
- mirror_map: int32 [8, 1536], replicated, may hold values from 0 to 1535, as said below
- pair_virt: int32 [8, 2, 1536], P(('bra', 'ket')), may hold values from 0 to 2047, as said below
- vir_energy: float32 [2048], replicated, may hold values from 0.1 to 1.5
- pair_energy: float32 [1536], P('pair'), may hold values from -1.5 to -0.4
Outputs:
- new_amplitudes: bfloat16 [1536, 8, 1536], P('pair', ('bra', 'ket'))
Inputs may be any that keep to these rules, and one draw needn't show every extreme that they name: `block_owner`: the 4 entries of a row are distinct. `mirror_map`: every row is a permutation of 0 to 1535, and row t + 4 is the inverse permutation of row t. `pair_virt`: if position p of tile t < 4 holds the orbitals (a, b), position mirror_map[t, p] of tile t + 4 holds (b, a).
All inputs are finite; a program needn't handle non-finite values.
Results may differ from a plain program's by a relative error of at most 0.0045.
Values may be sent and summed in bfloat16 or wider, within the bound.
A program may use at most 64 MiB of HBM per device.

v0:
```python
import jax
import jax.numpy as jnp
from jax import lax
from jax.sharding import PartitionSpec as P


def partner(block, axis, apart):
    count = lax.axis_size(axis)
    route = []
    for low in range(count):
        high = low | 1 << apart
        if high != low and high < count:
            route += [(low, high), (high, low)]
    return lax.ppermute(block, axis, route)


def permute_columns(tile_data, indices):
    return jnp.take(tile_data, indices, axis=1)


def local(
    amplitudes, integrals, screen_list, block_owner, mirror_map, pair_virt, vir_energy, pair_energy
):
    owners = lax.axis_size(("bra", "ket"))
    half_tiles = owners // 2
    mirror_bit = owners.bit_length() - 2
    self_index = lax.axis_index(("bra", "ket"))
    is_upper = self_index >= half_tiles
    folded_index = self_index % half_tiles
    map_lower = lax.dynamic_index_in_dim(mirror_map, folded_index, 0, keepdims=False)
    map_upper = lax.dynamic_index_in_dim(mirror_map, folded_index + half_tiles, 0, keepdims=False)
    own_tile = amplitudes[:, 0, :]
    rows_dev, block_len = own_tile.shape
    seg_width = integrals.shape[2]
    seg_count = block_len // seg_width
    partner_tile = partner(own_tile, ("bra", "ket"), mirror_bit)
    lower_raw = jnp.where(is_upper, partner_tile, own_tile)
    upper_raw = jnp.where(is_upper, own_tile, partner_tile)
    sym_fold = (
        (lower_raw.astype(jnp.float32) + permute_columns(upper_raw, map_lower).astype(jnp.float32))
        * 0.5
    ).astype(jnp.bfloat16)
    anti_fold = (
        (upper_raw.astype(jnp.float32) - permute_columns(lower_raw, map_upper).astype(jnp.float32))
        * 0.5
    ).astype(jnp.bfloat16)
    wanted_owner = block_owner[0]
    wanted_segment = screen_list[0]
    sender_ids = jnp.arange(owners, dtype=jnp.int32)
    matches = wanted_owner[None, :] == sender_ids[:, None]
    request = jnp.sum(jnp.where(matches, wanted_segment[None, :] + 1, 0), axis=1) - 1
    requested = lax.all_to_all(
        request[:, None], ("bra", "ket"), split_axis=0, concat_axis=0, tiled=True
    )[:, 0]
    receiver_upper = (sender_ids >= half_tiles).astype(jnp.int32)
    slot_index = receiver_upper * seg_count + jnp.maximum(requested, 0)
    folded_both = jnp.concatenate(
        [
            sym_fold.reshape(rows_dev, seg_count, seg_width),
            anti_fold.reshape(rows_dev, seg_count, seg_width),
        ],
        axis=1,
    )
    outgoing = jnp.take(folded_both, slot_index, axis=1)
    incoming = lax.all_to_all(outgoing, ("bra", "ket"), split_axis=1, concat_axis=1, tiled=True)
    operand = jnp.take(incoming, wanted_owner, axis=1).reshape(rows_dev, -1)
    arrived = lax.all_gather(integrals, "pair", axis=1, tiled=True)
    block_count = arrived.shape[1]
    flat_piece = arrived.reshape(block_count * seg_width, block_len)
    ladder = jnp.dot(operand, flat_piece, preferred_element_type=jnp.float32)
    partner_ladder = partner(ladder.astype(jnp.bfloat16), ("bra", "ket"), mirror_bit).astype(
        ladder.dtype
    )
    own_map = jnp.where(is_upper, map_upper, map_lower)
    direction = jnp.where(is_upper, 1.0, -1.0).astype(jnp.float32)
    residual = ladder + direction * permute_columns(partner_ladder, own_map)
    energy_first = jnp.take(vir_energy, pair_virt[0, 0])
    energy_second = jnp.take(vir_energy, pair_virt[0, 1])
    denominator = pair_energy[:, None] - energy_first[None, :] - energy_second[None, :]
    updated = own_tile.astype(jnp.float32) + residual / denominator
    return updated.astype(jnp.bfloat16)[:, None, :]


def solution(mesh):
    placed = (
        P("pair", ("bra", "ket"), None),
        P(("bra", "ket"), "pair", None, None),
        P(("bra", "ket"), None),
        P(("bra", "ket"), None),
        P(),
        P(("bra", "ket"), None, None),
        P(),
        P("pair"),
    )
    return jax.shard_map(
        local,
        mesh=mesh,
        in_specs=placed,
        out_specs=P("pair", ("bra", "ket"), None),
        check_vma=False,
    )
```

profile of v0, /device:TPU:0, one launch (start us, length us, event | category | flops | bytes accessed | tf_op | source)
XLA Modules:
  0.0 202.0 jit_solution(7439391696442257985)
XLA Ops:
  6.5 0.0 copy-start
  6.5 4.1 %collective-permute-start = (bf16[384,1536]{1,0:T(8,128)(2,1)}, bf16[384,1536]{1,0:T(8,128)(2,1)S(1)}, u32[]{:S(2)}, u32[]{:S(2)}) collective-permute-start(bf16[384,1536]{1,0:T(8,128)(2,1)} %bitcast.52), channel_id=1, source_target_pairs={{0,16},{16,0},{4,20},{20,4},{8,24},{24,8},{12,28},{28,12},{1,17},{... | collective-permute-start | bytes 3538952 | tf_op jit(solution)/shard_map/ppermute | solution.py:14
  10.6 0.7 add_bitcast_fusion.1
  11.3 0.7 select_reduce_fusion
  12.0 0.7 copy.62
  12.7 3.8 %all-to-all-start = ((s32[8,1,1]{2,1,0:T(1,128)}), s32[8,1,1]{2,1,0:T(1,128)S(1)}, u32[]{:S(2)}, u32[]{:S(2)}) async-start(s32[8,1,1]{2,1,0:T(1,128)} %copy.62), calls=%async_computation | async-start | bytes 8192 | tf_op jit(solution)/shard_map/all_to_all | solution.py:52
  16.5 0.0 all-gather.2.cloned.1.call-start
  16.5 0.7 all-gather.2.cloned.1.call-update
  17.2 0.9 dynamic-slice_reduce_fusion.1
  18.2 0.6 pad_clamp_fusion.4
  18.8 0.6 compare_and_fusion.2
  19.4 43.7 %all-to-all-done = s32[8,1,1]{2,1,0:T(1,128)S(1)} async-done(((s32[8,1,1]{2,1,0:T(1,128)}), s32[8,1,1]{2,1,0:T(1,128)S(1)}, u32[]{:S(2)}, u32[]{:S(2)}) %all-to-all-start) | async-done | bytes 64 | tf_op jit(solution)/shard_map/all_to_all | solution.py:52
  63.1 0.2 maximum_reduce_fusion
  63.4 0.6 pad_clamp_fusion.6
  64.0 0.5 compare_and_fusion.3
  64.5 0.0 collective-permute-done
  64.5 1.0 copy-done.5
  65.5 1.5 broadcast_select_fusion
  67.0 0.7 copy.63
  67.7 4.8 %gather_fusion.3 = bf16[1536,384]{1,0:T(8,128)(2,1)S(1)} fusion(bf16[384,1536]{0,1:T(8,128)(2,1)S(1)} %copy.63, s32[2048]{0:T(1024)} %pad_clamp_fusion.4), kind=kCustom, calls=%fused_computation.clone | custom fusion | bytes 2365440 | tf_op jit(solution)/shard_map/jit(_take)/gather | solution.py:18
  72.6 0.0 copy-start.2
  72.6 1.5 copy.64
  74.0 0.0 copy-done.2
  74.0 3.3 %multiply_convert_fusion.1 = (bf16[384,1536]{1,0:T(8,128)(2,1)}, bf16[384,1536]{1,0:T(8,128)(2,1)}) fusion(bf16[1536,384]{0,1:T(8,128)(2,1)} %copy.64, pred[1536]{0:T(1024)(128)(4,1)} %get-tuple-element.14, bf16[384,1536]{1,0:T(8,128)(2,1)} %copy-done.5, bf16[384,1,1536]{2,0,1:T(8,128)(2,1)S(1)} %copy-done.2, pred[]{:T(512)S(6)} %ge.53), kind=kLoop, calls=%fused_computation.13 | loop fusion | flops 4128768 | bytes 5899777 | tf_op jit(solution)/shard_map/convert_element_type | solution.py:42
  77.3 1.7 copy.66
  79.0 5.3 %gather_fusion.4 = bf16[1536,384]{1,0:T(8,128)(2,1)} fusion(bf16[384,1536]{0,1:T(8,128)(2,1)S(1)} %copy.66, s32[2048]{0:T(1024)S(1)} %pad_clamp_fusion.3), kind=kCustom, calls=%fused_computation.2.clone | custom fusion | bytes 2365440 | tf_op jit(solution)/shard_map/jit(_take)/gather | solution.py:18
  84.3 1.6 copy.67
  85.9 0.0 copy-done.8
  85.9 1.4 multiply_convert_fusion
  87.4 1.7 copy.68
  89.1 0.0 copy-start.3
  89.1 1.5 copy.70
  90.6 0.0 copy-done.3
  90.6 0.7 copy.65
  91.3 0.0 copy-start.4
  91.3 1.4 copy.69
  92.7 0.0 copy-done.4
  92.8 2.9 %pad_maximum_fusion = bf16[384,24,128]{2,0,1:T(8,128)(2,1)} fusion(bf16[384,12,128]{2,0,1:T(8,128)(2,1)S(1)} %copy-done.4, bf16[384,12,128]{2,0,1:T(8,128)(2,1)} %copy.69), kind=kLoop, calls=%fused_computation.7 | loop fusion | flops 1179648 | bytes 4718592 | tf_op jit(solution)/shard_map/concatenate | solution.py:57
  95.6 2.5 %gather_fusion = bf16[8,384,128]{2,1,0:T(8,128)(2,1)S(1)} fusion(bf16[384,24,128]{2,0,1:T(8,128)(2,1)} %pad_maximum_fusion, s32[1024]{0:T(1024)} %pad_clamp_fusion.6), kind=kCustom, calls=%fused_computation.4 | custom fusion | bytes 1572896 | tf_op jit(solution)/shard_map/jit(_take)/gather | solution.py:64
  98.1 0.0 copy-done.9
  98.1 1.0 select_bitcast_fusion
  99.2 5.4 %all-to-all-start.1 = ((bf16[384,8,128]{2,0,1:T(8,128)(2,1)}), bf16[384,8,128]{2,0,1:T(8,128)(2,1)S(1)}, u32[]{:S(2)}, u32[]{:S(2)}) async-start(bf16[384,8,128]{2,0,1:T(8,128)(2,1)} %select_bitcast_fusion), calls=%async_computation.1 | async-start | bytes 1572864 | tf_op jit(solution)/shard_map/all_to_all | solution.py:65
  104.5 0.0 copy-done.10
  104.6 20.3 %all-to-all-done.1 = bf16[384,8,128]{2,0,1:T(8,128)(2,1)S(1)} async-done(((bf16[384,8,128]{2,0,1:T(8,128)(2,1)}), bf16[384,8,128]{2,0,1:T(8,128)(2,1)S(1)}, u32[]{:S(2)}, u32[]{:S(2)}) %all-to-all-start.1) | async-done | bytes 786464 | tf_op jit(solution)/shard_map/all_to_all | solution.py:65
  124.8 0.6 gather_fusion.1
  125.4 0.1 select_bitcast_fusion.1
  125.6 0.2 copy.71
  125.8 0.0 all-gather.2.cloned.1.call-done
  125.8 0.0 copy-start.7
  125.8 3.6 %fusion.10 = (bf16[384,1536]{1,0:T(8,128)(2,1)S(1)}, f32[384,1536]{1,0:T(8,128)}) fusion(bf16[384,512]{0,1:T(8,128)(2,1)S(1)} %bitcast.55, bf16[512,1536]{1,0:T(8,128)(2,1)} %bitcast.56), kind=kOutput, calls=%fused_computation.61 | convolution fusion | flops 604569600 | bytes 5505024 | tf_op jit(solution)/shard_map/dot_general | solution.py:70
  129.4 0.0 collective-permute-start.1
  129.4 0.0 copy-done.7
  129.5 0.0 copy-done
  129.5 8.4 %gather_fusion.5 = f32[1536]{0:T(1024)S(1)} fusion(f32[2048]{0:T(1024)S(1)} %copy-done, s32[2048]{0:T(1024)S(1)} %pad_clamp_fusion.1), kind=kCustom, calls=%fused_computation.1.clone | custom fusion | bytes 18432 | tf_op jit(solution)/shard_map/jit(_take)/gather | solution.py:77
  137.9 8.4 %gather_fusion.6 = f32[1536]{0:T(1024)S(1)} fusion(f32[2048]{0:T(1024)S(1)} %copy-done, s32[2048]{0:T(1024)S(1)} %pad_clamp_fusion), kind=kCustom, calls=%fused_computation.3.clone | custom fusion | bytes 18432 | tf_op jit(solution)/shard_map/jit(_take)/gather | solution.py:78
  146.3 0.9 fusion.4
  147.3 0.6 and_select_fusion.1
  147.9 0.6 and_select_fusion
  148.5 33.4 %collective-permute-done.1 = bf16[384,1536]{1,0:T(8,128)(2,1)} collective-permute-done((bf16[384,1536]{1,0:T(8,128)(2,1)S(1)}, bf16[384,1536]{1,0:T(8,128)(2,1)}, u32[]{:S(2)}, u32[]{:S(2)}) %collective-permute-start.1) | collective-permute-done | bytes 1179680 | tf_op jit(solution)/shard_map/ppermute | solution.py:14
  181.9 1.6 copy.73
  183.5 4.8 %gather_fusion.2 = f32[1536,384]{1,0:T(8,128)} fusion(f32[384,1536]{0,1:T(8,128)S(1)} %copy.73, s32[2048]{0:T(1024)S(1)} %pad_clamp_fusion.2), kind=kCustom, calls=%fused_computation.6 | custom fusion | bytes 4724736 | tf_op jit(solution)/shard_map/jit(_take)/gather | solution.py:18
  188.3 3.3 %copy.74 = f32[1536,384]{0,1:T(8,128)} copy(f32[1536,384]{1,0:T(8,128)} %gather_fusion.2) | data formatting | bytes 4718592 | tf_op jit(solution)/shard_map/jit(_take)/gather | solution.py:18
  191.6 0.0 copy-done.1
  191.6 3.5 %fusion.3 = bf16[384,1,1536]{2,0,1:T(8,128)(2,1)} fusion(f32[1536]{0:T(1024)} %and_select_fusion, f32[1536]{0:T(1024)S(1)} %copy-done.6, f32[384]{0:T(512)} %param.19, f32[384,1536]{1,0:T(8,128)S(1)} %copy-done.1, f32[1536,384]{0,1:T(8,128)} %copy.74, pred[1536]{0:T(1024)(128)(4,1)} %get-tuple-element.13, f32[]{:T(128)S(6)} %select_n.154, ...), kind=kLoop, calls=%fused_computation.16 | loop fusion | flops 5308416 | bytes 7093252 | tf_op jit(solution)/shard_map/broadcast_in_dim | solution.py:81
  (19 shorter events, 0.1 us)
Async XLA Ops:
  6.5 123.0 %copy-start = (f32[2048]{0:T(1024)S(1)}, f32[2048]{0:T(1024)}, u32[]{:S(2)}) copy-start(f32[2048]{0:T(1024)} %param.18) | copy-start | bytes 24580
  6.5 57.9 %collective-permute-start = (bf16[384,1536]{1,0:T(8,128)(2,1)}, bf16[384,1536]{1,0:T(8,128)(2,1)S(1)}, u32[]{:S(2)}, u32[]{:S(2)}) collective-permute-start(bf16[384,1536]{1,0:T(8,128)(2,1)} %bitcast.52), channel_id=1, source_target_pairs={{0,16},{16,0},{4,20},{20,4},{8,24},{24,8},{12,28},{28,12},{1,17},{... | collective-permute-start | bytes 3538952 | tf_op jit(solution)/shard_map/ppermute | solution.py:14
  12.7 50.5 %all-to-all-start = ((s32[8,1,1]{2,1,0:T(1,128)}), s32[8,1,1]{2,1,0:T(1,128)S(1)}, u32[]{:S(2)}, u32[]{:S(2)}) async-start(s32[8,1,1]{2,1,0:T(1,128)} %copy.62), calls=%async_computation | async-start | bytes 8192 | tf_op jit(solution)/shard_map/all_to_all | solution.py:52
  16.5 109.3 %all-gather.2.cloned.1.call-start = ((), (), s32[]{:S(2)}) async-start(), calls=%async_computation.2 | async-start | bytes 1966080 | tf_op jit(solution)/shard_map/all_gather | solution.py:67
  64.5 1.0 copy-start.5
  72.6 1.5 copy-start.2
  84.3 1.6 copy-start.8
  89.1 1.5 copy-start.3
  91.3 1.5 copy-start.4
  95.6 2.5 %copy-start.9 = (pred[8]{0:T(512)(128)(4,1)S(1)}, pred[8]{0:T(512)(128)(4,1)}, u32[]{:S(2)}) copy-start(pred[8]{0:T(512)(128)(4,1)} %compare_and_fusion.3) | copy-start | bytes 28
  99.2 5.4 %copy-start.10 = (s32[1,4]{1,0:T(1,128)S(1)}, s32[1,4]{1,0:T(1,128)}, u32[]{:S(2)}) copy-start(s32[1,4]{1,0:T(1,128)} %param.15) | copy-start | bytes 52
  99.2 25.6 %all-to-all-start.1 = ((bf16[384,8,128]{2,0,1:T(8,128)(2,1)}), bf16[384,8,128]{2,0,1:T(8,128)(2,1)S(1)}, u32[]{:S(2)}, u32[]{:S(2)}) async-start(bf16[384,8,128]{2,0,1:T(8,128)(2,1)} %select_bitcast_fusion), calls=%async_computation.1 | async-start | bytes 1572864 | tf_op jit(solution)/shard_map/all_to_all | solution.py:65
  125.8 3.6 %copy-start.7 = (s32[1,2,1536]{2,1,0:T(2,128)S(1)}, s32[1,2,1536]{2,1,0:T(2,128)}, u32[]{:S(2)}) copy-start(s32[1,2,1536]{2,1,0:T(2,128)} %param.17) | copy-start | bytes 36868
  129.4 52.4 %collective-permute-start.1 = (bf16[384,1536]{1,0:T(8,128)(2,1)S(1)}, bf16[384,1536]{1,0:T(8,128)(2,1)}, u32[]{:S(2)}, u32[]{:S(2)}) collective-permute-start(bf16[384,1536]{1,0:T(8,128)(2,1)S(1)} %get-tuple-element.16), channel_id=1, source_target_pairs={{0,16},{16,0},{4,20},{20,4},{8,24},{24,8},{12,28},{28,12},{1,17},{... | collective-permute-start | bytes 3538952 | tf_op jit(solution)/shard_map/ppermute | solution.py:14
  188.3 3.3 %copy-start.1 = (f32[384,1536]{1,0:T(8,128)S(1)}, f32[384,1536]{1,0:T(8,128)}, u32[]{:S(2)}) copy-start(f32[384,1536]{1,0:T(8,128)} %get-tuple-element.17) | copy-start | bytes 7077892
  188.3 3.3 %copy-start.6 = (f32[1536]{0:T(1024)S(1)}, f32[1536]{0:T(1024)}, u32[]{:S(2)}) copy-start(f32[1536]{0:T(1024)} %and_select_fusion.1) | copy-start | bytes 18436
Sparse Core Ops, SparseCore 0:
  18.9 21.0 all-gather.1
where the time goes:
time: 203 us; the launch traced here: 202 us
  waiting for transfers between devices  98.1 us (48%)
  local copies, waits for them, and re-layouts  53.4 us (26%)
  other arithmetic  19.9 us (10%)
  between operations  13.7 us (7%)
  starting transfers between devices  13.3 us (7%)
  matrix products  3.62 us (2%)
    all_to_all x1, waiting for transfers between devices, local(): lax.all_to_all(request[:, None], ('bra', 'ket'), split_axis=0, concat_axi...  43.7 us
    ppermute x2, waiting for transfers between devices, partner(): return lax.ppermute(block, axis, route)  33.4 us
    gather x6, local copies, waits for them, and re-layouts, permute_columns(): return jnp.take(tile_data, indices, axis=1)  21.3 us
    all_to_all x1, waiting for transfers between devices, local(): lax.all_to_all(outgoing, ('bra', 'ket'), split_axis=1, concat_axis=1, til...  20.3 us
    gather x1, local copies, waits for them, and re-layouts, local(): energy_second = jnp.take(vir_energy, pair_virt[0, 1])  8.39 us
    gather x1, local copies, waits for them, and re-layouts, local(): energy_first = jnp.take(vir_energy, pair_virt[0, 0])  8.39 us
    all_to_all x1, starting transfers between devices, local(): lax.all_to_all(outgoing, ('bra', 'ket'), split_axis=1, concat_axis=1, til...  5.35 us
    ppermute x2, starting transfers between devices, partner(): return lax.ppermute(block, axis, route)  4.07 us
  transfers between devices with their start and end apart: 5, of which 3 were waited for; matrix products, arithmetic and copies ran while one was open for 29% of the time, Pallas kernels for 0%

commit v1 on v0

v1 whole, which is shorter than its diff:
```python
import functools

import jax
import jax.numpy as jnp
from jax import lax
from jax.experimental import pallas as pl
from jax.experimental.pallas import tpu as pltpu
from jax.sharding import PartitionSpec as P

OWNERS = ("bra", "ket")
VMEM = pltpu.VMEM
SMEM = pltpu.SMEM


def swap(block, axis, bit):
    count = lax.axis_size(axis)
    return lax.ppermute(block, axis, [(i, i ^ bit) for i in range(count)])


def column_step(length):
    return next(step for step in (512, 256, 128, length) if length % step == 0)


def params(limit=48 << 20):
    return pltpu.CompilerParams(vmem_limit_bytes=limit)


def select_kernel(seg_width, segs_ref, tile_ref, col_a_ref, col_b_ref, out_ref):
    dest = pl.program_id(0)
    length = tile_ref.shape[1]
    lane = lax.broadcasted_iota(jnp.int32, (length, seg_width), 1)
    hots = []
    for sub in range(4):
        col = (col_a_ref, col_b_ref)[sub // 2]
        base = segs_ref[dest * 4 + sub] * seg_width
        hots.append((col[...] == lane + base).astype(jnp.float32).astype(jnp.bfloat16))
    hot = jnp.concatenate(hots, axis=1)
    out_ref[0] = jnp.dot(tile_ref[...], hot, preferred_element_type=jnp.float32).astype(
        jnp.bfloat16
    )


def select_segments(tile, col_a, col_b, segs, seg_width):
    rows, length = tile.shape
    dests = segs.shape[0] // 4
    return pl.pallas_call(
        functools.partial(select_kernel, seg_width),
        grid=(dests,),
        in_specs=[
            pl.BlockSpec(memory_space=SMEM),
            pl.BlockSpec((rows, length), lambda d: (0, 0)),
            pl.BlockSpec((length, 1), lambda d: (0, 0)),
            pl.BlockSpec((length, 1), lambda d: (0, 0)),
        ],
        out_specs=pl.BlockSpec((1, rows, 4 * seg_width), lambda d: (d, 0, 0)),
        out_shape=jax.ShapeDtypeStruct((dests, rows, 4 * seg_width), jnp.bfloat16),
        compiler_params=params(),
        cost_estimate=pl.CostEstimate(
            flops=2 * rows * length * 4 * seg_width * dests,
            bytes_accessed=2 * rows * (length + dests * 4 * seg_width),
            transcendentals=0,
        ),
    )(segs, tile, col_a, col_b)


def permute_kernel(sign_ref, block_ref, col_ref, out_ref):
    step = out_ref.shape[1]
    length = block_ref.shape[1]
    lane = lax.broadcasted_iota(jnp.int32, (length, step), 1) + pl.program_id(0) * step
    hot = (col_ref[...] == lane).astype(jnp.float32).astype(jnp.bfloat16)
    moved = jnp.dot(block_ref[...], hot, preferred_element_type=jnp.float32)
    out_ref[...] = (moved * sign_ref[0]).astype(jnp.bfloat16)


def permute_block(block, col, sign):
    rows, length = block.shape
    step = column_step(length)
    return pl.pallas_call(
        permute_kernel,
        grid=(length // step,),
        in_specs=[
            pl.BlockSpec(memory_space=SMEM),
            pl.BlockSpec((rows, length), lambda j: (0, 0)),
            pl.BlockSpec((length, 1), lambda j: (0, 0)),
        ],
        out_specs=pl.BlockSpec((rows, step), lambda j: (0, j)),
        out_shape=jax.ShapeDtypeStruct((rows, length), jnp.bfloat16),
        compiler_params=params(),
        cost_estimate=pl.CostEstimate(
            flops=2 * rows * length * length, bytes_accessed=4 * rows * length, transcendentals=0
        ),
    )(sign, block, col)


def energy_kernel(table_ref, index_ref, out_ref):
    count = table_ref.shape[1]
    step = out_ref.shape[1]
    value = table_ref[...]
    high = value.astype(jnp.bfloat16)
    rest = value - high.astype(jnp.float32)
    middle = rest.astype(jnp.bfloat16)
    low = (rest - middle.astype(jnp.float32)).astype(jnp.bfloat16)
    spot = lax.broadcasted_iota(jnp.int32, (count, step), 0)
    for row in range(2):
        hot = (spot == index_ref[row : row + 1, :]).astype(jnp.float32).astype(jnp.bfloat16)
        parts = [
            jnp.dot(piece, hot, preferred_element_type=jnp.float32)
            for piece in (high, middle, low)
        ]
        out_ref[row : row + 1, :] = (parts[0][0:1] + parts[1][0:1]) + parts[2][0:1]


def pair_energies(vir_energy, index):
    count = vir_energy.shape[0]
    length = index.shape[1]
    step = column_step(length)
    table = jnp.broadcast_to(vir_energy[None, :], (8, count))
    return pl.pallas_call(
        energy_kernel,
        grid=(length // step,),
        in_specs=[
            pl.BlockSpec((8, count), lambda j: (0, 0)),
            pl.BlockSpec((2, step), lambda j: (0, j)),
        ],
        out_specs=pl.BlockSpec((2, step), lambda j: (0, j)),
        out_shape=jax.ShapeDtypeStruct((2, length), jnp.float32),
        compiler_params=params(),
        cost_estimate=pl.CostEstimate(
            flops=2 * 256 * count * length * 2, bytes_accessed=4 * count * 8, transcendentals=0
        ),
    )(table, index)


def assemble_kernel(source_ref, sub_ref, in_ref, out_ref):
    out_ref[...] = in_ref[0]


def assemble(messages, source, sub, seg_width):
    rows = messages.shape[1]
    slots = source.shape[0]
    return pl.pallas_call(
        assemble_kernel,
        grid_spec=pltpu.PrefetchScalarGridSpec(
            num_scalar_prefetch=2,
            grid=(slots,),
            in_specs=[
                pl.BlockSpec((1, rows, seg_width), lambda j, src, sub: (src[j], 0, sub[j]))
            ],
            out_specs=pl.BlockSpec((rows, seg_width), lambda j, src, sub: (0, j)),
        ),
        out_shape=jax.ShapeDtypeStruct((rows, slots * seg_width), jnp.bfloat16),
        compiler_params=params(),
        cost_estimate=pl.CostEstimate(
            flops=0, bytes_accessed=4 * rows * slots * seg_width, transcendentals=0
        ),
    )(source, sub, messages)


def final_kernel(
    pieces, flag_ref, mine_ref, recv_ref, tile_ref, pair_ref, vir_ref, *rest
):
    blocks = rest[: 2 * pieces]
    out_ref, own_ref, other_ref = rest[2 * pieces :]
    width = own_ref.shape[1]

    @pl.when(pl.program_id(0) == 0)
    def _():
        upper = flag_ref[0] > 0
        mine_a = mine_ref[:, :width].astype(jnp.float32)
        recv_a = recv_ref[:, :width].astype(jnp.float32)
        mine_b = mine_ref[:, width:].astype(jnp.float32)
        recv_b = recv_ref[:, width:].astype(jnp.float32)
        sym = ((mine_a + recv_a) * 0.5).astype(jnp.bfloat16)
        sign = jnp.where(upper, 0.5, -0.5).astype(jnp.float32)
        anti = ((mine_b - recv_b) * sign).astype(jnp.bfloat16)

        @pl.when(upper)
        def _():
            own_ref[...] = anti
            other_ref[...] = sym

        @pl.when(jnp.logical_not(upper))
        def _():
            own_ref[...] = sym
            other_ref[...] = anti

    depth = blocks[0].shape[0]
    total = None
    for held, part in ((own_ref, blocks[:pieces]), (other_ref, blocks[pieces:])):
        for at, block in enumerate(part):
            term = jnp.dot(
                held[:, at * depth : (at + 1) * depth],
                block[...],
                preferred_element_type=jnp.float32,
            )
            total = term if total is None else total + term
    denominator = pair_ref[...] - vir_ref[0:1, :] - vir_ref[1:2, :]
    out_ref[...] = (tile_ref[...].astype(jnp.float32) + total / denominator).astype(jnp.bfloat16)


def finish(flag, mine, recv, tile, pair_energy, energies, own_blocks, mirror_blocks):
    rows, length = tile.shape
    width = mine.shape[1] // 2
    step = 256 if length % 256 == 0 else column_step(length)
    pieces = len(own_blocks)
    depth = own_blocks[0].shape[0]
    whole = lambda j: (0, 0)
    across = lambda j: (0, j)
    return pl.pallas_call(
        functools.partial(final_kernel, pieces),
        grid=(length // step,),
        in_specs=[
            pl.BlockSpec(memory_space=SMEM),
            pl.BlockSpec(mine.shape, whole),
            pl.BlockSpec(recv.shape, whole),
            pl.BlockSpec((rows, step), across),
            pl.BlockSpec((rows, 1), whole),
            pl.BlockSpec((2, step), across),
        ]
        + [pl.BlockSpec((depth, step), across)] * (2 * pieces),
        out_specs=pl.BlockSpec((rows, step), across),
        out_shape=jax.ShapeDtypeStruct((rows, length), jnp.bfloat16),
        scratch_shapes=[VMEM((rows, width), jnp.bfloat16)] * 2,
        compiler_params=params(56 << 20),
        cost_estimate=pl.CostEstimate(
            flops=4 * rows * width * length,
            bytes_accessed=4 * (rows * length + width * length),
            transcendentals=0,
        ),
    )(flag, mine, recv, tile, pair_energy[:, None], energies, *own_blocks, *mirror_blocks)


def gather_pieces(block):
    pieces = [block]
    bit = lax.axis_size("pair") // 2
    order = [0]
    while bit:
        pieces += [swap(piece, "pair", bit) for piece in pieces]
        order += [at ^ bit for at in order]
        bit //= 2
    return pieces, order


def local(
    amplitudes, integrals, screen_list, block_owner, mirror_map, pair_virt, vir_energy, pair_energy
):
    owners = lax.axis_size(OWNERS)
    half = owners // 2
    self_index = lax.axis_index(OWNERS)
    upper = self_index >= half
    folded = self_index % half
    tile = amplitudes[:, 0, :]
    rows, length = tile.shape
    per, seg_width = integrals.shape[1:3]
    count = block_owner.shape[1]

    table = jnp.concatenate([block_owner, screen_list], axis=1)
    table = lax.all_to_all(
        jnp.broadcast_to(table, (owners, 2 * count)), OWNERS, split_axis=0, concat_axis=0, tiled=True
    )
    all_owner, all_screen = table[:, :count], table[:, count:]

    map_col = lax.dynamic_index_in_dim(mirror_map, self_index, 0, keepdims=False)[:, None]
    straight = lax.broadcasted_iota(jnp.int32, (length, 1), 0)
    col_a = jnp.where(upper, map_col, straight)
    col_b = jnp.where(upper, straight, map_col)
    shard = integrals[0].reshape(per * seg_width, length)
    sign = jnp.where(upper, -1.0, 1.0).astype(jnp.float32)[None]
    own_blocks, order = gather_pieces(shard)
    mirror_shard = swap(permute_block(shard, map_col, sign), OWNERS, half)
    mirror_blocks, _ = gather_pieces(mirror_shard)

    step = jnp.arange(half, dtype=jnp.int32)
    tiles = (folded ^ step)[:, None] + jnp.array([0, half], jnp.int32)[None, :]
    tile_hot = tiles[:, :, None] == jnp.arange(owners, dtype=jnp.int32)
    dest_owner = jnp.sum(jnp.where(tile_hot[..., None], all_owner, 0), axis=2)
    dest_screen = jnp.sum(jnp.where(tile_hot[..., None], all_screen, 0), axis=2)
    serving = folded + jnp.array([0, half], jnp.int32)
    match = dest_owner[:, :, None, :] == serving[None, None, :, None]
    segs = jnp.sum(jnp.where(match, dest_screen[:, :, None, :], 0), axis=3).reshape(-1)

    outgoing = select_segments(tile, col_a, col_b, segs, seg_width)
    messages = [outgoing[0]] + [swap(outgoing[d], OWNERS, d) for d in range(1, half)]

    pair_at = lax.axis_index("pair")
    slot = (
        jnp.concatenate([(pair_at ^ at) * per + jnp.arange(per, dtype=jnp.int32) for at in order])
    )
    slot_hot = slot[:, None] == jnp.arange(count, dtype=jnp.int32)[None, :]
    mine_owner = jnp.sum(jnp.where(slot_hot[None], dest_owner[0][:, None, :], 0), axis=2)
    source = ((mine_owner % half) ^ folded).reshape(-1)
    sub = (mine_owner // half + jnp.array([[0], [2]], jnp.int32)).reshape(-1)
    mine = assemble(jnp.stack(messages), source, sub, seg_width)
    recv = swap(mine, OWNERS, half)

    energies = pair_energies(vir_energy, pair_virt[0])
    flag = upper.astype(jnp.int32)[None]
    updated = finish(flag, mine, recv, tile, pair_energy, energies, own_blocks, mirror_blocks)
    return updated[:, None, :]


def solution(mesh):
    placed = (
        P("pair", OWNERS, None),
        P(OWNERS, "pair", None, None),
        P(OWNERS, None),
        P(OWNERS, None),
        P(),
        P(OWNERS, None, None),
        P(),
        P("pair"),
    )
    return jax.shard_map(
        local,
        mesh=mesh,
        in_specs=placed,
        out_specs=P("pair", OWNERS, None),
        check_vma=False,
    )
```

time: 203 us -> 97.1 us (0.48)
  waiting for transfers between devices: 98.1 us -> 49.6 us
  local copies, waits for them, and re-layouts: 53.4 us -> 6.15 us
  Pallas kernels: 0 us -> 20.4 us
  other arithmetic: 19.9 us -> 2.98 us
  between operations: 13.7 us -> 0.23 us
  starting transfers between devices: 13.3 us -> 17.4 us
  matrix products: 3.62 us -> 0 us
    all_to_all x2 -> x1, waiting for transfers between devices: 64 us -> 0.01 us  [local(): lax.all_to_all(jnp.broadcast_to(table, (owners, 2 * count)), OWNERS, spli...]
    gather x10 -> x0, local copies, waits for them, and re-layouts: 41.2 us -> none  [the longest x6 21.3 us: permute_columns(): return jnp.take(tile_data, indices, axis=1)]
    pallas_call x0 -> x5, Pallas kernels: none -> 20.4 us  [the longest x1 7.7 us: finish(): pl.pallas_call(functools.partial(final_kernel, pieces), grid=(length // s...]
    ppermute x2 -> x11, waiting for transfers between devices: 33.4 us -> 49.6 us  [swap(): return lax.ppermute(block, axis, [(i, i ^ bit) for i in range(count)])]
    ppermute x2 -> x11, starting transfers between devices: 4.07 us -> 10.1 us  [swap(): return lax.ppermute(block, axis, [(i, i ^ bit) for i in range(count)])]
    convert_element_type x2 -> x0, other arithmetic: 4.74 us -> none  [the longest x1 3.29 us: local(): sym_fold = ((lower_raw.astype(jnp.float32) + permute_columns(upper_raw, m...]
    broadcast_in_dim x2 -> x0, other arithmetic: 4.2 us -> none  [the longest x1 3.55 us: local(): return updated.astype(jnp.bfloat16)[:, None, :]]
    convert_element_type x3 -> x0, local copies, waits for them, and re-layouts: 3.99 us -> none  [the longest x1 1.7 us: local(): anti_fold = ((upper_raw.astype(jnp.float32) - permute_columns(lower_raw,...]
  transfers between devices with their start and end apart: 5 -> 12, of which waited for: 3 -> 5; matrix products, arithmetic and copies ran while one was open for 29% -> 4% of each run, Pallas kernels for 0% -> 13%
where the time goes in v1:
time: 97.1 us; the launch traced here: 96.7 us
  waiting for transfers between devices  49.6 us (51%)
  Pallas kernels  20.4 us (21%)
  starting transfers between devices  17.4 us (18%)
  local copies, waits for them, and re-layouts  6.15 us (6%)
  other arithmetic  2.98 us (3%)
    ppermute x11, waiting for transfers between devices, swap(): return lax.ppermute(block, axis, [(i, i ^ bit) for i in range(count)])  49.6 us
    ppermute x11, starting transfers between devices, swap(): return lax.ppermute(block, axis, [(i, i ^ bit) for i in range(count)])  10.1 us
    pallas_call x1, Pallas kernels, finish(): pl.pallas_call(functools.partial(final_kernel, pieces), grid=(length // s...  7.7 us
    all_to_all x1, starting transfers between devices, local(): lax.all_to_all(jnp.broadcast_to(table, (owners, 2 * count)), OWNERS, spli...  7.31 us
    pallas_call x1, Pallas kernels, pair_energies(): pl.pallas_call(energy_kernel, grid=(length // step,), in_specs=[pl.BlockS...  6.02 us
    pallas_call x1, Pallas kernels, select_segments(): pl.pallas_call(functools.partial(select_kernel, seg_width), grid=(dests,)...  4.16 us
    unnamed x26, local copies, waits for them, and re-layouts  3.67 us
  transfers between devices with their start and end apart: 12, of which 5 were waited for; matrix products, arithmetic and copies ran while one was open for 4% of the time, Pallas kernels for 13%

profile of v1, /device:TPU:0, one launch (start us, length us, event | category | flops | bytes accessed | tf_op | source)
XLA Modules:
  0.0 96.7 jit_solution(16725994774151601243)
XLA Ops:
  0.0 0.8 add_bitcast_fusion
  0.8 0.6 broadcast_in_dim.101
  1.4 7.3 %all-to-all-start = ((s32[8,1,8]{2,1,0:T(1,128)}), s32[8,1,8]{2,1,0:T(1,128)S(1)}, u32[]{:S(2)}, u32[]{:S(2)}) async-start(s32[8,1,8]{2,1,0:T(1,128)} %broadcast_in_dim.101), calls=%async_computation | async-start | bytes 8192 | tf_op jit(solution)/shard_map/all_to_all | solution.py:258
  8.7 1.5 %collective-permute-start.4 = (bf16[128,1536]{1,0:T(8,128)(2,1)}, bf16[128,1536]{1,0:T(8,128)(2,1)}, u32[]{:S(2)}, u32[]{:S(2)}) collective-permute-start(bf16[128,1536]{1,0:T(8,128)(2,1)} %bitcast.28), channel_id=1, source_target_pairs={{0,2},{1,3},{2,0},{3,1},{4,6},{5,7},{6,4},{7,5},{8,10},{9,11},{10,... | collective-permute-start | bytes 1179656 | tf_op jit(solution)/shard_map/ppermute | solution.py:17
  10.2 0.0 copy-done
  10.2 0.3 copy.25.col_ref
  10.5 0.0 copy-start.4
  10.5 1.0 %copy-done.4 = bf16[1,1,128,1536]{3,2,1,0:T(8,128)(2,1)S(1)} copy-done((bf16[1,1,128,1536]{3,2,1,0:T(8,128)(2,1)S(1)}, bf16[1,1,128,1536]{3,2,1,0:T(8,128)(2,1)}, u32[]{:S(2)}) %copy-start.4) | copy-done | bytes 393240
  11.5 1.4 %shard_map.112 = bf16[128,1536]{1,0:T(8,128)(2,1)S(1)} custom-call(f32[1]{0:T(128)} %bitcast.18.sign_ref, bf16[128,1536]{1,0:T(8,128)(2,1)S(1)} %bitcast.30, s32[1536,1]{1,0:T(8,128)S(1)} %copy.25.col_ref), custom_call_target="tpu_custom_call" | custom-call | flops 603979776 | bytes 786432 | tf_op jit(solution)/shard_map/pallas_call | solution.py:78
  12.9 0.0 copy-start.2
  12.9 3.0 %collective-permute-start.7 = (bf16[128,1536]{1,0:T(8,128)(2,1)S(1)}, bf16[128,1536]{1,0:T(8,128)(2,1)}, u32[]{:S(2)}, u32[]{:S(2)}) collective-permute-start(bf16[128,1536]{1,0:T(8,128)(2,1)S(1)} %shard_map.112), channel_id=1, source_target_pairs={{0,16},{4,20},{8,24},{12,28},{16,0},{20,4},{24,8},{28,12},{1,17},{... | collective-permute-start | bytes 1179656 | tf_op jit(solution)/shard_map/ppermute | solution.py:17
  15.9 1.0 %iota_select_fusion = (s32[1536,1]{1,0:T(8,128)S(1)}, s32[1536,1]{1,0:T(8,128)}) fusion(s32[1536,1]{1,0:T(8,128)S(1)} %copy.25.col_ref, pred[]{:T(512)S(6)} %ge.3), kind=kLoop, calls=%fused_computation.1 | loop fusion | flops 3072 | bytes 18433 | tf_op jit(solution)/shard_map/jit(_where)/select_n | solution.py:266
  16.9 0.1 broadcast_add_fusion
  16.9 0.1 iota_compare_fusion
  17.0 0.1 pad_add_fusion
  17.1 0.1 iota_compare_fusion.1
  17.2 0.1 add.79
  17.3 0.1 add.80
  17.3 0.0 all-to-all-done
  17.3 0.1 fusion.3
  17.4 0.1 copy.20
  17.5 0.1 copy.22
  17.6 0.4 select_reduce_fusion
  18.0 0.2 select_reduce_fusion.2
  18.2 0.1 copy.24
  18.3 0.1 reshape.103.segs_ref
  18.4 0.0 copy-start.3
  18.4 1.1 %copy-done.3 = s32[1536,1]{1,0:T(8,128)S(1)} copy-done((s32[1536,1]{1,0:T(8,128)S(1)}, s32[1536,1]{1,0:T(8,128)}, u32[]{:S(2)}) %copy-start.3) | copy-done | bytes 6168
  19.5 4.2 %shard_map.109 = bf16[4,384,512]{2,1,0:T(8,128)(2,1)S(1)} custom-call(s32[16]{0:T(128)S(1)} %reshape.103.segs_ref, bf16[384,1536]{1,0:T(8,128)(2,1)S(1)} %bitcast.27, s32[1536,1]{1,0:T(8,128)S(1)} %copy-done.3, s32[1536,1]{1,0:T(8,128)S(1)} %get-tuple-element.11.col_b_ref), custom_call_target="tpu_custom_call" | custom-call | flops 2415919104 | bytes 2752512 | tf_op jit(solution)/shard_map/pallas_call | solution.py:46
  23.7 0.1 fusion.2
  23.8 1.5 %collective-permute-start = (bf16[384,512]{1,0:T(8,128)(2,1)S(1)}, bf16[384,512]{1,0:T(8,128)(2,1)S(1)}, u32[]{:S(2)}, u32[]{:S(2)}) collective-permute-start(bf16[384,512]{1,0:T(8,128)(2,1)S(1)} %get-tuple-element.10), channel_id=1, source_target_pairs={{0,4},{4,0},{8,12},{12,8},{16,20},{20,16},{24,28},{28,24},{1,5},{5... | collective-permute-start | bytes 1179656 | tf_op jit(solution)/shard_map/ppermute | solution.py:17
  25.3 1.5 %collective-permute-start.1 = (bf16[384,512]{1,0:T(8,128)(2,1)S(1)}, bf16[384,512]{1,0:T(8,128)(2,1)S(1)}, u32[]{:S(2)}, u32[]{:S(2)}) collective-permute-start(bf16[384,512]{1,0:T(8,128)(2,1)S(1)} %get-tuple-element.9), channel_id=1, source_target_pairs={{0,8},{4,12},{8,0},{12,4},{16,24},{20,28},{24,16},{28,20},{1,9},{5... | collective-permute-start | bytes 1179656 | tf_op jit(solution)/shard_map/ppermute | solution.py:17
  26.8 0.6 collective-permute-start.2
  27.3 0.1 select_reduce_fusion.3
  27.5 0.1 reduce_sum.40
  27.6 5.2 %collective-permute-done.7.rest_4_ = bf16[128,1536]{1,0:T(8,128)(2,1)} collective-permute-done((bf16[128,1536]{1,0:T(8,128)(2,1)S(1)}, bf16[128,1536]{1,0:T(8,128)(2,1)}, u32[]{:S(2)}, u32[]{:S(2)}) %collective-permute-start.7) | collective-permute-done | bytes 393248 | tf_op jit(solution)/shard_map/ppermute | solution.py:17
  32.8 0.5 collective-permute-start.8
  33.3 0.3 collective-permute-done
  33.6 7.5 %collective-permute-done.1 = bf16[384,512]{1,0:T(8,128)(2,1)S(1)} collective-permute-done((bf16[384,512]{1,0:T(8,128)(2,1)S(1)}, bf16[384,512]{1,0:T(8,128)(2,1)S(1)}, u32[]{:S(2)}, u32[]{:S(2)}) %collective-permute-start.1) | collective-permute-done | bytes 393248 | tf_op jit(solution)/shard_map/ppermute | solution.py:17
  41.1 9.5 %collective-permute-done.2 = bf16[384,512]{1,0:T(8,128)(2,1)S(1)} collective-permute-done((bf16[384,512]{1,0:T(8,128)(2,1)S(1)}, bf16[384,512]{1,0:T(8,128)(2,1)S(1)}, u32[]{:S(2)}, u32[]{:S(2)}) %collective-permute-start.2) | collective-permute-done | bytes 393248 | tf_op jit(solution)/shard_map/ppermute | solution.py:17
  50.6 0.2 pad_maximum_fusion.in_ref
  50.8 0.0 copy-start.5
  50.8 0.0 copy-start.12
  50.8 0.0 copy-start.11
  50.8 0.0 copy-start.7
  50.8 1.1 %shard_map.110.mine_ref = bf16[384,1024]{1,0:T(8,128)(2,1)S(1)} custom-call(s32[8]{0:T(128)S(1)} %get-tuple-element.16.source_ref, s32[8]{0:T(128)S(1)} %get-tuple-element.15.sub_ref, bf16[4,384,512]{2,1,0:T(8,128)(2,1)S(1)} %pad_maximum_fusion.in_ref), custom_call_target="tpu_custom_call" | custom-call | bytes 1572864 | tf_op jit(solution)/shard_map/pallas_call | solution.py:141
  52.0 0.5 collective-permute-start.3
  52.5 0.0 copy-done.5
  52.5 0.0 collective-permute-start.5
  52.5 0.5 collective-permute-start.9
  53.0 0.0 collective-permute-done.4.rest_1_
  53.0 0.0 collective-permute-start.6
  53.0 0.0 collective-permute-done.8.rest_5_
  53.0 0.5 collective-permute-start.10
  53.5 0.8 broadcast_in_dim.116.pair_ref
  54.4 6.0 %shard_map.111.vir_ref = f32[2,1536]{1,0:T(2,128)S(1)} custom-call(f32[8,2048]{1,0:T(8,128)S(1)} %broadcast_in_dim.112.table_ref, s32[2,1536]{1,0:T(2,128)S(1)} %bitcast.32), custom_call_target="tpu_custom_call" | custom-call | flops 3221225472 | bytes 65536 | tf_op jit(solution)/shard_map/pallas_call | solution.py:118
  60.4 0.6 copy-done.6
  61.0 0.0 collective-permute-done.5.rest_2_
  61.0 0.0 collective-permute-done.9.rest_6_
  61.0 0.0 collective-permute-done.6.rest_3_
  61.0 0.0 collective-permute-done.10.rest_7_
  61.0 27.1 %collective-permute-done.3.recv_ref = bf16[384,1024]{1,0:T(8,128)(2,1)S(1)} collective-permute-done((bf16[384,1024]{1,0:T(8,128)(2,1)S(1)}, bf16[384,1024]{1,0:T(8,128)(2,1)S(1)}, u32[]{:S(2)}, u32[]{:S(2)}) %collective-permute-start.3) | collective-permute-done | bytes 786464 | tf_op jit(solution)/shard_map/ppermute | solution.py:17
  88.1 0.9 copy-done.8
  89.0 7.7 %shard_map.113 = bf16[384,1536]{1,0:T(8,128)(2,1)} custom-call(s32[1]{0:T(128)} %bitcast.flag_ref, bf16[384,1024]{1,0:T(8,128)(2,1)} %copy-done.1, bf16[384,1024]{1,0:T(8,128)(2,1)} %copy-done.8, bf16[384,1536]{1,0:T(8,128)(2,1)} %bitcast.26, f32[384,1]{1,0:T(8,128)} %broadcast_in_dim.116.pair_ref, f32[2,1536]{1,0:T(2,128)} %copy-done.6, ...), custom_call_target="tpu_custom_call" | custom-call | flops 1207959552 | bytes 5505024 | tf_op jit(solution)/shard_map/pallas_call | solution.py:209
  (23 shorter events, 0.1 us)
Async XLA Ops:
  0.0 10.2 %copy-start = (s32[8,1536]{1,0:T(8,128)S(1)}, s32[8,1536]{1,0:T(8,128)}, u32[]{:S(2)}) copy-start(s32[8,1536]{1,0:T(8,128)} %param.15) | copy-start | bytes 147460
  1.4 16.0 %all-to-all-start = ((s32[8,1,8]{2,1,0:T(1,128)}), s32[8,1,8]{2,1,0:T(1,128)S(1)}, u32[]{:S(2)}, u32[]{:S(2)}) async-start(s32[8,1,8]{2,1,0:T(1,128)} %broadcast_in_dim.101), calls=%async_computation | async-start | bytes 8192 | tf_op jit(solution)/shard_map/all_to_all | solution.py:258
  8.7 44.3 %collective-permute-start.4 = (bf16[128,1536]{1,0:T(8,128)(2,1)}, bf16[128,1536]{1,0:T(8,128)(2,1)}, u32[]{:S(2)}, u32[]{:S(2)}) collective-permute-start(bf16[128,1536]{1,0:T(8,128)(2,1)} %bitcast.28), channel_id=1, source_target_pairs={{0,2},{1,3},{2,0},{3,1},{4,6},{5,7},{6,4},{7,5},{8,10},{9,11},{10,... | collective-permute-start | bytes 1179656 | tf_op jit(solution)/shard_map/ppermute | solution.py:17
  10.5 1.0 %copy-start.4 = (bf16[1,1,128,1536]{3,2,1,0:T(8,128)(2,1)S(1)}, bf16[1,1,128,1536]{3,2,1,0:T(8,128)(2,1)}, u32[]{:S(2)}) copy-start(bf16[1,1,128,1536]{3,2,1,0:T(8,128)(2,1)} %param.12) | copy-start | bytes 1179652
  12.9 5.5 %copy-start.2 = (bf16[384,1,1536]{2,0,1:T(8,128)(2,1)S(1)}, bf16[384,1,1536]{2,0,1:T(8,128)(2,1)}, u32[]{:S(2)}) copy-start(bf16[384,1,1536]{2,0,1:T(8,128)(2,1)} %param.11) | copy-start | bytes 3538948
  12.9 19.9 %collective-permute-start.7 = (bf16[128,1536]{1,0:T(8,128)(2,1)S(1)}, bf16[128,1536]{1,0:T(8,128)(2,1)}, u32[]{:S(2)}, u32[]{:S(2)}) collective-permute-start(bf16[128,1536]{1,0:T(8,128)(2,1)S(1)} %shard_map.112), channel_id=1, source_target_pairs={{0,16},{4,20},{8,24},{12,28},{16,0},{20,4},{24,8},{28,12},{1,17},{... | collective-permute-start | bytes 1179656 | tf_op jit(solution)/shard_map/ppermute | solution.py:17
  18.4 1.1 %copy-start.3 = (s32[1536,1]{1,0:T(8,128)S(1)}, s32[1536,1]{1,0:T(8,128)}, u32[]{:S(2)}) copy-start(s32[1536,1]{1,0:T(8,128)} %get-tuple-element.12.col_a_ref) | copy-start | bytes 18436
  23.8 9.8 %collective-permute-start = (bf16[384,512]{1,0:T(8,128)(2,1)S(1)}, bf16[384,512]{1,0:T(8,128)(2,1)S(1)}, u32[]{:S(2)}, u32[]{:S(2)}) collective-permute-start(bf16[384,512]{1,0:T(8,128)(2,1)S(1)} %get-tuple-element.10), channel_id=1, source_target_pairs={{0,4},{4,0},{8,12},{12,8},{16,20},{20,16},{24,28},{28,24},{1,5},{5... | collective-permute-start | bytes 1179656 | tf_op jit(solution)/shard_map/ppermute | solution.py:17
  25.3 15.8 %collective-permute-start.1 = (bf16[384,512]{1,0:T(8,128)(2,1)S(1)}, bf16[384,512]{1,0:T(8,128)(2,1)S(1)}, u32[]{:S(2)}, u32[]{:S(2)}) collective-permute-start(bf16[384,512]{1,0:T(8,128)(2,1)S(1)} %get-tuple-element.9), channel_id=1, source_target_pairs={{0,8},{4,12},{8,0},{12,4},{16,24},{20,28},{24,16},{28,20},{1,9},{5... | collective-permute-start | bytes 1179656 | tf_op jit(solution)/shard_map/ppermute | solution.py:17
  26.8 23.8 %collective-permute-start.2 = (bf16[384,512]{1,0:T(8,128)(2,1)S(1)}, bf16[384,512]{1,0:T(8,128)(2,1)S(1)}, u32[]{:S(2)}, u32[]{:S(2)}) collective-permute-start(bf16[384,512]{1,0:T(8,128)(2,1)S(1)} %get-tuple-element.8), channel_id=1, source_target_pairs={{0,12},{4,8},{8,4},{12,0},{16,28},{20,24},{24,20},{28,16},{1,13},{... | collective-permute-start | bytes 1179656 | tf_op jit(solution)/shard_map/ppermute | solution.py:17
  32.8 20.2 %collective-permute-start.8 = (bf16[128,1536]{1,0:T(8,128)(2,1)}, bf16[128,1536]{1,0:T(8,128)(2,1)S(1)}, u32[]{:S(2)}, u32[]{:S(2)}) collective-permute-start(bf16[128,1536]{1,0:T(8,128)(2,1)} %collective-permute-done.7.rest_4_), channel_id=1, source_target_pairs={{0,2},{1,3},{2,0},{3,1},{4,6},{5,7},{6,4},{7,5},{8,10},{9,11},{10,... | collective-permute-start | bytes 1179656 | tf_op jit(solution)/shard_map/ppermute | solution.py:17
  50.8 1.7 %copy-start.5 = (bf16[1,1,128,1536]{3,2,1,0:T(8,128)(2,1)S(1)}, bf16[1,1,128,1536]{3,2,1,0:T(8,128)(2,1)}, u32[]{:S(2)}) copy-start(bf16[1,1,128,1536]{3,2,1,0:T(8,128)(2,1)} %param.12) | copy-start | bytes 1179652
  50.8 2.7 %copy-start.12 = (f32[384]{0:T(512)S(1)}, f32[384]{0:T(512)}, u32[]{:S(2)}) copy-start(f32[384]{0:T(512)} %param.18) | copy-start | bytes 4612
  50.8 3.5 %copy-start.11 = (f32[2048]{0:T(1024)S(1)}, f32[2048]{0:T(1024)}, u32[]{:S(2)}) copy-start(f32[2048]{0:T(1024)} %param.17) | copy-start | bytes 24580
  50.8 3.5 %copy-start.7 = (s32[1,2,1536]{2,1,0:T(2,128)S(1)}, s32[1,2,1536]{2,1,0:T(2,128)}, u32[]{:S(2)}) copy-start(s32[1,2,1536]{2,1,0:T(2,128)} %param.16) | copy-start | bytes 36868
  51.9 8.4 %copy-start.1 = (bf16[384,1024]{1,0:T(8,128)(2,1)}, bf16[384,1024]{1,0:T(8,128)(2,1)S(1)}, u32[]{:S(2)}) copy-start(bf16[384,1024]{1,0:T(8,128)(2,1)S(1)} %shard_map.110.mine_ref) | copy-start | bytes 2359300
  52.0 36.2 %collective-permute-start.3 = (bf16[384,1024]{1,0:T(8,128)(2,1)S(1)}, bf16[384,1024]{1,0:T(8,128)(2,1)S(1)}, u32[]{:S(2)}, u32[]{:S(2)}) collective-permute-start(bf16[384,1024]{1,0:T(8,128)(2,1)S(1)} %shard_map.110.mine_ref), channel_id=1, source_target_pairs={{0,16},{4,20},{8,24},{12,28},{16,0},{20,4},{24,8},{28,12},{1,17},{... | collective-permute-start | bytes 2359304 | tf_op jit(solution)/shard_map/ppermute | solution.py:17
  52.5 8.5 %collective-permute-start.5 = (bf16[128,1536]{1,0:T(8,128)(2,1)S(1)}, bf16[128,1536]{1,0:T(8,128)(2,1)S(1)}, u32[]{:S(2)}, u32[]{:S(2)}) collective-permute-start(bf16[128,1536]{1,0:T(8,128)(2,1)S(1)} %bitcast.31), channel_id=1, source_target_pairs={{0,1},{1,0},{2,3},{3,2},{4,5},{5,4},{6,7},{7,6},{8,9},{9,8},{10,11... | collective-permute-start | bytes 1179656 | tf_op jit(solution)/shard_map/ppermute | solution.py:17
  52.5 8.5 %collective-permute-start.9 = (bf16[128,1536]{1,0:T(8,128)(2,1)}, bf16[128,1536]{1,0:T(8,128)(2,1)}, u32[]{:S(2)}, u32[]{:S(2)}) collective-permute-start(bf16[128,1536]{1,0:T(8,128)(2,1)} %collective-permute-done.7.rest_4_), channel_id=1, source_target_pairs={{0,1},{1,0},{2,3},{3,2},{4,5},{5,4},{6,7},{7,6},{8,9},{9,8},{10,11... | collective-permute-start | bytes 1179656 | tf_op jit(solution)/shard_map/ppermute | solution.py:17
  53.0 8.0 %collective-permute-start.6 = (bf16[128,1536]{1,0:T(8,128)(2,1)}, bf16[128,1536]{1,0:T(8,128)(2,1)}, u32[]{:S(2)}, u32[]{:S(2)}) collective-permute-start(bf16[128,1536]{1,0:T(8,128)(2,1)} %collective-permute-done.4.rest_1_), channel_id=1, source_target_pairs={{0,1},{1,0},{2,3},{3,2},{4,5},{5,4},{6,7},{7,6},{8,9},{9,8},{10,11... | collective-permute-start | bytes 1179656 | tf_op jit(solution)/shard_map/ppermute | solution.py:17
  53.0 7.4 %copy-start.9 = (bf16[128,1536]{1,0:T(8,128)(2,1)}, bf16[128,1536]{1,0:T(8,128)(2,1)S(1)}, u32[]{:S(2)}) copy-start(bf16[128,1536]{1,0:T(8,128)(2,1)S(1)} %collective-permute-done.8.rest_5_) | copy-start | bytes 1179652
  53.0 8.0 %collective-permute-start.10 = (bf16[128,1536]{1,0:T(8,128)(2,1)S(1)}, bf16[128,1536]{1,0:T(8,128)(2,1)}, u32[]{:S(2)}, u32[]{:S(2)}) collective-permute-start(bf16[128,1536]{1,0:T(8,128)(2,1)S(1)} %collective-permute-done.8.rest_5_), channel_id=1, source_target_pairs={{0,1},{1,0},{2,3},{3,2},{4,5},{5,4},{6,7},{7,6},{8,9},{9,8},{10,11... | collective-permute-start | bytes 1179656 | tf_op jit(solution)/shard_map/ppermute | solution.py:17
  60.4 0.6 copy-start.6
  61.0 27.1 %copy-start.10 = (bf16[128,1536]{1,0:T(8,128)(2,1)}, bf16[128,1536]{1,0:T(8,128)(2,1)S(1)}, u32[]{:S(2)}) copy-start(bf16[128,1536]{1,0:T(8,128)(2,1)S(1)} %collective-permute-done.5.rest_2_) | copy-start | bytes 1179652
  88.1 0.9 copy-start.8

commit v2 on v1

--- a/solution.py
+++ b/solution.py
@@ -8,6 +8,7 @@
 from jax.sharding import PartitionSpec as P
 
 OWNERS = ("bra", "ket")
+CHUNKS = 2
 VMEM = pltpu.VMEM
 SMEM = pltpu.SMEM
 
@@ -25,26 +26,90 @@
     return pltpu.CompilerParams(vmem_limit_bytes=limit)
 
 
-def select_kernel(seg_width, segs_ref, tile_ref, col_a_ref, col_b_ref, out_ref):
+def chunk_count(rows, half):
+    if half > 8:
+        return 1
+    return next(c for c in (CHUNKS, 3, 2, 1) if c == 1 or rows % (16 * c) == 0)
+
+
+def table_kernel(owners, ket, row_ref, out_ref, held, send_sem, recv_sem):
+    me = lax.axis_index(OWNERS)
+    peers = [me ^ d for d in range(owners)]
+    places = [{"bra": peer // ket, "ket": peer % ket} for peer in peers]
+    barrier = pltpu.get_barrier_semaphore()
+    for d in range(1, owners):
+        pl.semaphore_signal(
+            barrier, inc=1, device_id=places[d], device_id_type=pl.DeviceIdType.MESH
+        )
+    pl.semaphore_wait(barrier, owners - 1)
+    copies = []
+    for d in range(1, owners):
+        copy = pltpu.make_async_remote_copy(
+            src_ref=row_ref,
+            dst_ref=held.at[d],
+            send_sem=send_sem.at[d],
+            recv_sem=recv_sem.at[d],
+            device_id=places[d],
+            device_id_type=pl.DeviceIdType.MESH,
+        )
+        copy.start()
+        copies.append(copy)
+    out_ref[0:1, :] = row_ref[0:1, :]
+    for d in range(1, owners):
+        copies[d - 1].wait()
+        out_ref[d : d + 1, :] = held[d, 0:1, :]
+
+
+def exchange_tables(row):
+    owners = lax.axis_size(OWNERS)
+    width = row.shape[1]
+    return pl.pallas_call(
+        functools.partial(table_kernel, owners, lax.axis_size("ket")),
+        in_specs=[pl.BlockSpec(memory_space=VMEM)],
+        out_specs=pl.BlockSpec(memory_space=VMEM),
+        out_shape=jax.ShapeDtypeStruct((owners, width), jnp.int32),
+        scratch_shapes=[
+            VMEM((owners, 8, width), jnp.int32),
+            pltpu.SemaphoreType.DMA((owners,)),
+            pltpu.SemaphoreType.DMA((owners,)),
+        ],
+        compiler_params=pltpu.CompilerParams(
+            collective_id=1, has_side_effects=True, vmem_limit_bytes=8 << 20
+        ),
+    )(row)
+
+
+def select_kernel(count, seg_width, segs_ref, tile_ref, col_a_ref, col_b_ref, *out_refs):
     dest = pl.program_id(0)
+    half = pl.num_programs(0)
+    flip = segs_ref[0, 2 * count] * half
+    folded = segs_ref[0, 2 * count + 1]
     length = tile_ref.shape[1]
     lane = lax.broadcasted_iota(jnp.int32, (length, seg_width), 1)
     hots = []
     for sub in range(4):
         col = (col_a_ref, col_b_ref)[sub // 2]
-        base = segs_ref[dest * 4 + sub] * seg_width
+        row = dest + (flip if sub < 2 else half - flip)
+        serving = folded + (sub % 2) * half
+        segment = jnp.int32(0)
+        for k in range(count):
+            held = segs_ref[row, k] == serving
+            segment += jnp.where(held, segs_ref[row, count + k], 0)
+        base = segment * seg_width
         hots.append((col[...] == lane + base).astype(jnp.float32).astype(jnp.bfloat16))
     hot = jnp.concatenate(hots, axis=1)
-    out_ref[0] = jnp.dot(tile_ref[...], hot, preferred_element_type=jnp.float32).astype(
-        jnp.bfloat16
-    )
-
-
-def select_segments(tile, col_a, col_b, segs, seg_width):
+    part = out_refs[0].shape[1]
+    for at, out_ref in enumerate(out_refs):
+        out_ref[0] = jnp.dot(
+            tile_ref[at * part : (at + 1) * part, :], hot, preferred_element_type=jnp.float32
+        ).astype(jnp.bfloat16)
+
+
+def select_segments(tile, col_a, col_b, segs, count, seg_width, chunks):
     rows, length = tile.shape
-    dests = segs.shape[0] // 4
-    return pl.pallas_call(
-        functools.partial(select_kernel, seg_width),
+    dests = segs.shape[0] // 2
+    return pl.pallas_call(
+        functools.partial(select_kernel, count, seg_width),
         grid=(dests,),
         in_specs=[
             pl.BlockSpec(memory_space=SMEM),
@@ -52,8 +117,11 @@
             pl.BlockSpec((length, 1), lambda d: (0, 0)),
             pl.BlockSpec((length, 1), lambda d: (0, 0)),
         ],
-        out_specs=pl.BlockSpec((1, rows, 4 * seg_width), lambda d: (d, 0, 0)),
-        out_shape=jax.ShapeDtypeStruct((dests, rows, 4 * seg_width), jnp.bfloat16),
+        out_specs=[pl.BlockSpec((1, rows // chunks, 4 * seg_width), lambda d: (d, 0, 0))] * chunks,
+        out_shape=[
+            jax.ShapeDtypeStruct((dests, rows // chunks, 4 * seg_width), jnp.bfloat16)
+        ]
+        * chunks,
         compiler_params=params(),
         cost_estimate=pl.CostEstimate(
             flops=2 * rows * length * 4 * seg_width * dests,
@@ -160,7 +228,7 @@
     pieces, flag_ref, mine_ref, recv_ref, tile_ref, pair_ref, vir_ref, *rest
 ):
     blocks = rest[: 2 * pieces]
-    out_ref, own_ref, other_ref = rest[2 * pieces :]
+    out_ref, own_ref, other_ref = rest[-3:]
     width = own_ref.shape[1]
 
     @pl.when(pl.program_id(0) == 0)
@@ -185,25 +253,32 @@
             other_ref[...] = anti
 
     depth = blocks[0].shape[0]
-    total = None
-    for held, part in ((own_ref, blocks[:pieces]), (other_ref, blocks[pieces:])):
-        for at, block in enumerate(part):
-            term = jnp.dot(
-                held[:, at * depth : (at + 1) * depth],
-                block[...],
-                preferred_element_type=jnp.float32,
-            )
-            total = term if total is None else total + term
-    denominator = pair_ref[...] - vir_ref[0:1, :] - vir_ref[1:2, :]
-    out_ref[...] = (tile_ref[...].astype(jnp.float32) + total / denominator).astype(jnp.bfloat16)
-
-
-def finish(flag, mine, recv, tile, pair_energy, energies, own_blocks, mirror_blocks):
-    rows, length = tile.shape
+    step = column_step(out_ref.shape[1])
+    for start in range(0, out_ref.shape[1], step):
+        at_columns = slice(start, start + step)
+        total = None
+        for held, part in ((own_ref, blocks[:pieces]), (other_ref, blocks[pieces:])):
+            for at, block in enumerate(part):
+                term = jnp.dot(
+                    held[:, at * depth : (at + 1) * depth],
+                    block[:, at_columns],
+                    preferred_element_type=jnp.float32,
+                )
+                total = term if total is None else total + term
+        denominator = pair_ref[...] - vir_ref[0:1, at_columns] - vir_ref[1:2, at_columns]
+        raw = tile_ref[:, at_columns].astype(jnp.float32)
+        out_ref[:, at_columns] = (raw + total / denominator).astype(jnp.bfloat16)
+
+
+def finish(at, earlier, flag, mine, recv, tile, pair_energy, energies, own_blocks, mirror_blocks):
+    length = tile.shape[1]
+    rows = mine.shape[0]
     width = mine.shape[1] // 2
-    step = 256 if length % 256 == 0 else column_step(length)
     pieces = len(own_blocks)
     depth = own_blocks[0].shape[0]
+    small = 4 * pieces * depth * length <= 8 << 20
+    step = length if small else column_step(length) // 2
+    before = [] if earlier is None else [earlier]
     whole = lambda j: (0, 0)
     across = lambda j: (0, j)
     return pl.pallas_call(
@@ -213,13 +288,15 @@
             pl.BlockSpec(memory_space=SMEM),
             pl.BlockSpec(mine.shape, whole),
             pl.BlockSpec(recv.shape, whole),
-            pl.BlockSpec((rows, step), across),
-            pl.BlockSpec((rows, 1), whole),
+            pl.BlockSpec((rows, step), lambda j: (at, j)),
+            pl.BlockSpec((rows, 1), lambda j: (at, 0)),
             pl.BlockSpec((2, step), across),
         ]
-        + [pl.BlockSpec((depth, step), across)] * (2 * pieces),
-        out_specs=pl.BlockSpec((rows, step), across),
-        out_shape=jax.ShapeDtypeStruct((rows, length), jnp.bfloat16),
+        + [pl.BlockSpec((depth, step), across)] * (2 * pieces)
+        + [pl.BlockSpec(memory_space=pl.ANY)] * len(before),
+        out_specs=pl.BlockSpec((rows, step), lambda j: (at, j)),
+        out_shape=jax.ShapeDtypeStruct(tile.shape, jnp.bfloat16),
+        input_output_aliases={6 + 2 * pieces: 0} if before else {},
         scratch_shapes=[VMEM((rows, width), jnp.bfloat16)] * 2,
         compiler_params=params(56 << 20),
         cost_estimate=pl.CostEstimate(
@@ -227,7 +304,7 @@
             bytes_accessed=4 * (rows * length + width * length),
             transcendentals=0,
         ),
-    )(flag, mine, recv, tile, pair_energy[:, None], energies, *own_blocks, *mirror_blocks)
+    )(flag, mine, recv, tile, pair_energy[:, None], energies, *own_blocks, *mirror_blocks, *before)
 
 
 def gather_pieces(block):
@@ -254,48 +331,52 @@
     per, seg_width = integrals.shape[1:3]
     count = block_owner.shape[1]
 
-    table = jnp.concatenate([block_owner, screen_list], axis=1)
-    table = lax.all_to_all(
-        jnp.broadcast_to(table, (owners, 2 * count)), OWNERS, split_axis=0, concat_axis=0, tiled=True
+    row = jnp.concatenate(
+        [block_owner, screen_list, upper.astype(jnp.int32).reshape(1, 1), folded.reshape(1, 1)],
+        axis=1,
     )
-    all_owner, all_screen = table[:, :count], table[:, count:]
+    row = jnp.pad(row, ((0, 7), (0, -row.shape[1] % 128)))
+    table = exchange_tables(row)
 
     map_col = lax.dynamic_index_in_dim(mirror_map, self_index, 0, keepdims=False)[:, None]
     straight = lax.broadcasted_iota(jnp.int32, (length, 1), 0)
     col_a = jnp.where(upper, map_col, straight)
     col_b = jnp.where(upper, straight, map_col)
     shard = integrals[0].reshape(per * seg_width, length)
-    sign = jnp.where(upper, -1.0, 1.0).astype(jnp.float32)[None]
+    sign = jnp.where(upper, 1.0, -1.0).astype(jnp.float32)[None]
     own_blocks, order = gather_pieces(shard)
-    mirror_shard = swap(permute_block(shard, map_col, sign), OWNERS, half)
+    back_col = lax.dynamic_index_in_dim(
+        mirror_map, (self_index + half) % owners, 0, keepdims=False
+    )[:, None]
+    mirror_shard = permute_block(swap(shard, OWNERS, half), back_col, sign)
     mirror_blocks, _ = gather_pieces(mirror_shard)
 
-    step = jnp.arange(half, dtype=jnp.int32)
-    tiles = (folded ^ step)[:, None] + jnp.array([0, half], jnp.int32)[None, :]
-    tile_hot = tiles[:, :, None] == jnp.arange(owners, dtype=jnp.int32)
-    dest_owner = jnp.sum(jnp.where(tile_hot[..., None], all_owner, 0), axis=2)
-    dest_screen = jnp.sum(jnp.where(tile_hot[..., None], all_screen, 0), axis=2)
-    serving = folded + jnp.array([0, half], jnp.int32)
-    match = dest_owner[:, :, None, :] == serving[None, None, :, None]
-    segs = jnp.sum(jnp.where(match, dest_screen[:, :, None, :], 0), axis=3).reshape(-1)
-
-    outgoing = select_segments(tile, col_a, col_b, segs, seg_width)
-    messages = [outgoing[0]] + [swap(outgoing[d], OWNERS, d) for d in range(1, half)]
-
+    chunks = chunk_count(rows, half)
+    outgoing = select_segments(tile, col_a, col_b, table, count, seg_width, chunks)
     pair_at = lax.axis_index("pair")
     slot = (
         jnp.concatenate([(pair_at ^ at) * per + jnp.arange(per, dtype=jnp.int32) for at in order])
     )
     slot_hot = slot[:, None] == jnp.arange(count, dtype=jnp.int32)[None, :]
-    mine_owner = jnp.sum(jnp.where(slot_hot[None], dest_owner[0][:, None, :], 0), axis=2)
+    own_row, other_row = table[0, :count], table[half, :count]
+    dest_owner = jnp.stack(
+        [jnp.where(upper, other_row, own_row), jnp.where(upper, own_row, other_row)]
+    )
+    mine_owner = jnp.sum(jnp.where(slot_hot[None], dest_owner[:, None, :], 0), axis=2)
     source = ((mine_owner % half) ^ folded).reshape(-1)
     sub = (mine_owner // half + jnp.array([[0], [2]], jnp.int32)).reshape(-1)
-    mine = assemble(jnp.stack(messages), source, sub, seg_width)
-    recv = swap(mine, OWNERS, half)
-
     energies = pair_energies(vir_energy, pair_virt[0])
     flag = upper.astype(jnp.int32)[None]
-    updated = finish(flag, mine, recv, tile, pair_energy, energies, own_blocks, mirror_blocks)
+    updated = None
+    for at in range(chunks):
+        messages = [outgoing[at][0]] + [
+            swap(outgoing[at][d], OWNERS, d) for d in range(1, half)
+        ]
+        mine = assemble(jnp.stack(messages), source, sub, seg_width)
+        recv = swap(mine, OWNERS, half)
+        updated = finish(
+            at, updated, flag, mine, recv, tile, pair_energy, energies, own_blocks, mirror_blocks
+        )
     return updated[:, None, :]
 
 

time: 97.1 us -> 92 us (0.947)
  waiting for transfers between devices: 49.6 us -> 35.7 us
  Pallas kernels: 20.4 us -> 32.2 us
  starting transfers between devices: 17.4 us -> 14.6 us
  other arithmetic: 2.98 us -> 1.63 us
  local copies, waits for them, and re-layouts: 6.15 us -> 7.3 us
    ppermute x11 -> x15, waiting for transfers between devices: 49.6 us -> 35.7 us  [swap(): return lax.ppermute(block, axis, [(i, i ^ bit) for i in range(count)])]
    pallas_call x1 -> x2, Pallas kernels: 4.16 us -> 13.5 us  [the longest x1 8.6 us: exchange_tables(): pl.pallas_call(functools.partial(table_kernel, owners, lax.axis_size('ket...]
    all_to_all x1 -> x0, starting transfers between devices: 7.31 us -> none  [local(): lax.all_to_all(jnp.broadcast_to(table, (owners, 2 * count)), OWNERS, spli...]
    ppermute x11 -> x15, starting transfers between devices: 10.1 us -> 14.6 us  [swap(): return lax.ppermute(block, axis, [(i, i ^ bit) for i in range(count)])]
    pallas_call x1 -> x2, Pallas kernels: 7.7 us -> 9.38 us  [finish(): pl.pallas_call(functools.partial(final_kernel, pieces), grid=(length // s...]
    slice x4 -> x2, local copies, waits for them, and re-layouts: 0.34 us -> 1.67 us  [local(): outgoing[at][0]]
    unnamed x26 -> x38, local copies, waits for them, and re-layouts: 3.67 us -> 3.06 us
  transfers between devices with their start and end apart: 12 -> 15, of which waited for: 5 -> 5; matrix products, arithmetic and copies ran while one was open for 4% -> 4% of each run, Pallas kernels for 13% -> 15%
where the time goes in v2:
time: 92 us; the launch traced here: 91.8 us
  waiting for transfers between devices  35.7 us (39%)
  Pallas kernels  32.2 us (35%)
  starting transfers between devices  14.6 us (16%)
  local copies, waits for them, and re-layouts  7.3 us (8%)
  other arithmetic  1.63 us (2%)
    ppermute x15, waiting for transfers between devices, swap(): return lax.ppermute(block, axis, [(i, i ^ bit) for i in range(count)])  35.7 us
    ppermute x15, starting transfers between devices, swap(): return lax.ppermute(block, axis, [(i, i ^ bit) for i in range(count)])  14.6 us
    pallas_call x2, Pallas kernels, finish(): pl.pallas_call(functools.partial(final_kernel, pieces), grid=(length // s...  9.38 us
    pallas_call x1, Pallas kernels, exchange_tables(): pl.pallas_call(functools.partial(table_kernel, owners, lax.axis_size('ket...  8.6 us
    pallas_call x1, Pallas kernels, pair_energies(): pl.pallas_call(energy_kernel, grid=(length // step,), in_specs=[pl.BlockS...  6.02 us
    pallas_call x1, Pallas kernels, select_segments(): pl.pallas_call(functools.partial(select_kernel, count, seg_width), grid=(...  4.88 us
    unnamed x38, local copies, waits for them, and re-layouts  3.06 us
    pallas_call x2, Pallas kernels, assemble(): pl.pallas_call(assemble_kernel, grid_spec=pltpu.PrefetchScalarGridSpec(nu...  1.9 us
  transfers between devices with their start and end apart: 15, of which 5 were waited for; matrix products, arithmetic and copies ran while one was open for 4% of the time, Pallas kernels for 15%

profile of v2, /device:TPU:0, one launch (start us, length us, event | category | flops | bytes accessed | tf_op | source)
XLA Modules:
  0.0 91.8 jit_solution(183290328097024571)
XLA Ops:
  0.0 0.9 dynamic-slice_bitcast_fusion
  0.9 0.3 copy.16
  1.2 0.0 copy-start.17
  1.2 0.0 copy-start.18
  1.2 0.0 copy-start
  1.2 0.1 iota_select_fusion
  1.4 0.5 copy-done.17
  1.9 0.0 copy-done.18
  1.9 0.1 pad_add_fusion.2
  2.0 8.6 %shard_map.91.segs_ref = s32[8,128]{1,0:T(8,128)S(1)} custom-call(s32[8,128]{1,0:T(8,128)S(1)} %pad.4.row_ref), custom_call_target="tpu_custom_call" | custom-call | tf_op jit(solution)/shard_map/pallas_call | solution.py:66
  10.6 4.9 %shard_map.92 = (bf16[4,192,512]{2,1,0:T(8,128)(2,1)S(1)}, bf16[4,192,512]{2,1,0:T(8,128)(2,1)S(1)}) custom-call(s32[8,128]{1,0:T(8,128)S(1)} %shard_map.91.segs_ref, bf16[384,1536]{1,0:T(8,128)(2,1)S(1)} %bitcast.36, s32[1536,1]{1,0:T(8,128)S(1)} %get-tuple-element.18.col_a_ref, s32[1536,1]{1,0:T(8,128)S(1)} %get-tuple-element.17.col_b_ref), custom_call_target="tpu_custom_call" | custom-call | flops 2415919104 | bytes 2752512 | tf_op jit(solution)/shard_map/pallas_call | solution.py:111
  15.5 0.0 copy-start.6
  15.5 0.9 fusion.2
  16.4 1.5 %collective-permute-start.11 = (bf16[192,512]{1,0:T(8,128)(2,1)}, bf16[192,512]{1,0:T(8,128)(2,1)S(1)}, u32[]{:S(2)}, u32[]{:S(2)}) collective-permute-start(bf16[192,512]{1,0:T(8,128)(2,1)} %get-tuple-element.12), channel_id=1, source_target_pairs={{0,4},{4,0},{8,12},{12,8},{16,20},{20,16},{24,28},{28,24},{1,5},{5... | collective-permute-start | bytes 589832 | tf_op jit(solution)/shard_map/ppermute | solution.py:18
  17.9 1.2 %collective-permute-start.12 = (bf16[192,512]{1,0:T(8,128)(2,1)}, bf16[192,512]{1,0:T(8,128)(2,1)S(1)}, u32[]{:S(2)}, u32[]{:S(2)}) collective-permute-start(bf16[192,512]{1,0:T(8,128)(2,1)} %get-tuple-element.11), channel_id=1, source_target_pairs={{0,8},{4,12},{8,0},{12,4},{16,24},{20,28},{24,16},{28,20},{1,9},{5... | collective-permute-start | bytes 589832 | tf_op jit(solution)/shard_map/ppermute | solution.py:18
  19.1 0.8 collective-permute-start.13
  19.8 2.2 %collective-permute-start.7 = (bf16[128,1536]{1,0:T(8,128)(2,1)S(1)}, bf16[128,1536]{1,0:T(8,128)(2,1)S(1)}, u32[]{:S(2)}, u32[]{:S(2)}) collective-permute-start(bf16[128,1536]{1,0:T(8,128)(2,1)S(1)} %bitcast.40), channel_id=1, source_target_pairs={{0,16},{4,20},{8,24},{12,28},{16,0},{20,4},{24,8},{28,12},{1,17},{... | collective-permute-start | bytes 1179656 | tf_op jit(solution)/shard_map/ppermute | solution.py:18
  22.1 0.8 fusion.3
  22.9 1.5 %collective-permute-start = (bf16[192,512]{1,0:T(8,128)(2,1)}, bf16[192,512]{1,0:T(8,128)(2,1)S(1)}, u32[]{:S(2)}, u32[]{:S(2)}) collective-permute-start(bf16[192,512]{1,0:T(8,128)(2,1)} %get-tuple-element.16), channel_id=1, source_target_pairs={{0,4},{4,0},{8,12},{12,8},{16,20},{20,16},{24,28},{28,24},{1,5},{5... | collective-permute-start | bytes 589832 | tf_op jit(solution)/shard_map/ppermute | solution.py:18
  24.4 0.1 pad_add_fusion.1
  24.4 0.1 iota_compare_fusion
  24.5 0.1 select_reduce_fusion
  24.7 0.3 copy.18.col_ref
  25.0 13.2 %collective-permute-done.7.block_ref = bf16[128,1536]{1,0:T(8,128)(2,1)S(1)} collective-permute-done((bf16[128,1536]{1,0:T(8,128)(2,1)S(1)}, bf16[128,1536]{1,0:T(8,128)(2,1)S(1)}, u32[]{:S(2)}, u32[]{:S(2)}) %collective-permute-start.7) | collective-permute-done | bytes 393248 | tf_op jit(solution)/shard_map/ppermute | solution.py:18
  38.2 1.5 %collective-permute-start.4 = (bf16[128,1536]{1,0:T(8,128)(2,1)S(1)}, bf16[128,1536]{1,0:T(8,128)(2,1)S(1)}, u32[]{:S(2)}, u32[]{:S(2)}) collective-permute-start(bf16[128,1536]{1,0:T(8,128)(2,1)S(1)} %bitcast.41), channel_id=1, source_target_pairs={{0,2},{1,3},{2,0},{3,1},{4,6},{5,7},{6,4},{7,5},{8,10},{9,11},{10,... | collective-permute-start | bytes 1179656 | tf_op jit(solution)/shard_map/ppermute | solution.py:18
  39.7 1.4 %shard_map.95.rest_4_ = bf16[128,1536]{1,0:T(8,128)(2,1)S(1)} custom-call(f32[1]{0:T(128)} %bitcast.17.sign_ref, bf16[128,1536]{1,0:T(8,128)(2,1)S(1)} %collective-permute-done.7.block_ref, s32[1536,1]{1,0:T(8,128)S(1)} %copy.18.col_ref), custom_call_target="tpu_custom_call" | custom-call | flops 603979776 | bytes 786432 | tf_op jit(solution)/shard_map/pallas_call | solution.py:146
  41.1 0.0 collective-permute-done.11
  41.1 0.6 collective-permute-start.8
  41.7 0.1 reduce_sum.12
  41.8 0.1 add.64
  41.9 0.1 add.65
  42.0 0.0 collective-permute-done.12
  42.0 0.0 collective-permute-start.5
  42.0 0.0 collective-permute-done.13
  42.0 0.3 collective-permute-start.1
  42.3 0.0 collective-permute-done
  42.3 2.7 %collective-permute-start.2 = (bf16[192,512]{1,0:T(8,128)(2,1)S(1)}, bf16[192,512]{1,0:T(8,128)(2,1)S(1)}, u32[]{:S(2)}, u32[]{:S(2)}) collective-permute-start(bf16[192,512]{1,0:T(8,128)(2,1)S(1)} %get-tuple-element.14), channel_id=1, source_target_pairs={{0,12},{4,8},{8,4},{12,0},{16,28},{20,24},{24,20},{28,16},{1,13},{... | collective-permute-start | bytes 589832 | tf_op jit(solution)/shard_map/ppermute | solution.py:18
  45.0 1.0 %pad_maximum_fusion.1.in_ref = bf16[4,192,512]{2,1,0:T(8,128)(2,1)S(1)} fusion(bf16[1,192,512]{2,1,0:T(8,128)(2,1)} %bitcast.24, bf16[1,192,512]{2,1,0:T(8,128)(2,1)S(1)} %bitcast.45, bf16[1,192,512]{2,1,0:T(8,128)(2,1)S(1)} %bitcast.44, bf16[1,192,512]{2,1,0:T(8,128)(2,1)S(1)} %get-tuple-element.9), kind=kLoop, calls=%fused_computation.1 | loop fusion | flops 1179648 | bytes 1572864 | tf_op jit(solution)/shard_map/stack | solution.py:375
  46.1 1.0 %shard_map.96.mine_ref = bf16[192,1024]{1,0:T(8,128)(2,1)S(1)} custom-call(s32[8]{0:T(128)S(1)} %get-tuple-element.24.source_ref, s32[8]{0:T(128)S(1)} %get-tuple-element.23.sub_ref, bf16[4,192,512]{2,1,0:T(8,128)(2,1)S(1)} %pad_maximum_fusion.1.in_ref), custom_call_target="tpu_custom_call" | custom-call | bytes 786432 | tf_op jit(solution)/shard_map/pallas_call | solution.py:209
  47.0 3.0 %collective-permute-done.1 = bf16[192,512]{1,0:T(8,128)(2,1)S(1)} collective-permute-done((bf16[192,512]{1,0:T(8,128)(2,1)}, bf16[192,512]{1,0:T(8,128)(2,1)S(1)}, u32[]{:S(2)}, u32[]{:S(2)}) %collective-permute-start.1) | collective-permute-done | bytes 196640 | tf_op jit(solution)/shard_map/ppermute | solution.py:18
  50.0 1.6 %collective-permute-start.14 = (bf16[192,1024]{1,0:T(8,128)(2,1)S(1)}, bf16[192,1024]{1,0:T(8,128)(2,1)S(1)}, u32[]{:S(2)}, u32[]{:S(2)}) collective-permute-start(bf16[192,1024]{1,0:T(8,128)(2,1)S(1)} %shard_map.96.mine_ref), channel_id=1, source_target_pairs={{0,16},{4,20},{8,24},{12,28},{16,0},{20,4},{24,8},{28,12},{1,17},{... | collective-permute-start | bytes 1179656 | tf_op jit(solution)/shard_map/ppermute | solution.py:18
  51.7 5.5 %collective-permute-done.2 = bf16[192,512]{1,0:T(8,128)(2,1)S(1)} collective-permute-done((bf16[192,512]{1,0:T(8,128)(2,1)S(1)}, bf16[192,512]{1,0:T(8,128)(2,1)S(1)}, u32[]{:S(2)}, u32[]{:S(2)}) %collective-permute-start.2) | collective-permute-done | bytes 196640 | tf_op jit(solution)/shard_map/ppermute | solution.py:18
  57.2 0.0 collective-permute-start.9
  57.2 0.0 collective-permute-done.4.rest_1_
  57.2 0.5 collective-permute-start.6
  57.7 0.0 collective-permute-done.8.rest_5_
  57.7 0.1 collective-permute-start.10
  57.8 0.1 pad_maximum_fusion.in_ref
  57.9 1.0 %shard_map.93.mine_ref = bf16[192,1024]{1,0:T(8,128)(2,1)S(1)} custom-call(s32[8]{0:T(128)S(1)} %get-tuple-element.24.source_ref, s32[8]{0:T(128)S(1)} %get-tuple-element.23.sub_ref, bf16[4,192,512]{2,1,0:T(8,128)(2,1)S(1)} %pad_maximum_fusion.in_ref), custom_call_target="tpu_custom_call" | custom-call | bytes 786432 | tf_op jit(solution)/shard_map/pallas_call | solution.py:209
  58.9 0.0 collective-permute-done.5.rest_2_
  58.9 0.1 collective-permute-start.3
  59.0 0.8 broadcast_in_dim.59.pair_ref
  59.9 6.0 %shard_map.94.vir_ref = f32[2,1536]{1,0:T(2,128)S(1)} custom-call(f32[8,2048]{1,0:T(8,128)S(1)} %broadcast_in_dim.55.table_ref, s32[2,1536]{1,0:T(2,128)S(1)} %bitcast.37), custom_call_target="tpu_custom_call" | custom-call | flops 3221225472 | bytes 65536 | tf_op jit(solution)/shard_map/pallas_call | solution.py:186
  65.9 0.6 copy-done.4
  66.5 13.3 %collective-permute-done.14.recv_ref = bf16[192,1024]{1,0:T(8,128)(2,1)S(1)} collective-permute-done((bf16[192,1024]{1,0:T(8,128)(2,1)S(1)}, bf16[192,1024]{1,0:T(8,128)(2,1)S(1)}, u32[]{:S(2)}, u32[]{:S(2)}) %collective-permute-start.14) | collective-permute-done | bytes 393248 | tf_op jit(solution)/shard_map/ppermute | solution.py:18
  79.8 0.0 collective-permute-done.6.rest_3_
  79.8 0.7 copy-done.14
  80.5 0.1 copy-done.10
  80.7 0.2 copy-done.11
  80.8 0.1 copy-done.12
  81.0 4.7 %shard_map.97.rest_8_ = bf16[384,1536]{1,0:T(8,128)(2,1)} custom-call(s32[1]{0:T(128)} %bitcast.flag_ref, bf16[192,1024]{1,0:T(8,128)(2,1)} %copy-done.3, bf16[192,1024]{1,0:T(8,128)(2,1)} %copy-done.14, bf16[384,1536]{1,0:T(8,128)(2,1)} %bitcast.34, f32[384,1]{1,0:T(8,128)} %broadcast_in_dim.59.pair_ref, f32[2,1536]{1,0:T(2,128)} %copy-done.4, ...), custom_call_target="tpu_custom_call" | custom-call | flops 603979776 | bytes 4325376 | tf_op jit(solution)/shard_map/pallas_call | solution.py:284
  85.6 0.7 collective-permute-done.3.recv_ref
  86.3 0.8 copy-done.13
  87.1 4.7 %shard_map.98 = bf16[384,1536]{1,0:T(8,128)(2,1)} custom-call(s32[1]{0:T(128)} %bitcast.flag_ref, bf16[192,1024]{1,0:T(8,128)(2,1)} %copy-done.2, bf16[192,1024]{1,0:T(8,128)(2,1)} %copy-done.13, bf16[384,1536]{1,0:T(8,128)(2,1)} %bitcast.35, f32[384,1]{1,0:T(8,128)} %broadcast_in_dim.59.pair_ref, ...), custom_call_target="tpu_custom_call", output_to_operand_aliasing={{}: (14, {})} | custom-call | flops 603979776 | bytes 4325376 | tf_op jit(solution)/shard_map/pallas_call | solution.py:284
  (34 shorter events, 0.1 us)
Async XLA Ops:
  1.2 0.7 copy-start.17
  1.2 0.7 copy-start.18
  1.2 9.3 %copy-start = (bf16[384,1,1536]{2,0,1:T(8,128)(2,1)S(1)}, bf16[384,1,1536]{2,0,1:T(8,128)(2,1)}, u32[]{:S(2)}) copy-start(bf16[384,1,1536]{2,0,1:T(8,128)(2,1)} %param.9) | copy-start | bytes 3538948
  15.5 4.4 %copy-start.6 = (bf16[1,1,128,1536]{3,2,1,0:T(8,128)(2,1)S(1)}, bf16[1,1,128,1536]{3,2,1,0:T(8,128)(2,1)}, u32[]{:S(2)}) copy-start(bf16[1,1,128,1536]{3,2,1,0:T(8,128)(2,1)} %param.10) | copy-start | bytes 1179652
  16.4 24.8 %collective-permute-start.11 = (bf16[192,512]{1,0:T(8,128)(2,1)}, bf16[192,512]{1,0:T(8,128)(2,1)S(1)}, u32[]{:S(2)}, u32[]{:S(2)}) collective-permute-start(bf16[192,512]{1,0:T(8,128)(2,1)} %get-tuple-element.12), channel_id=1, source_target_pairs={{0,4},{4,0},{8,12},{12,8},{16,20},{20,16},{24,28},{28,24},{1,5},{5... | collective-permute-start | bytes 589832 | tf_op jit(solution)/shard_map/ppermute | solution.py:18
  17.9 24.1 %collective-permute-start.12 = (bf16[192,512]{1,0:T(8,128)(2,1)}, bf16[192,512]{1,0:T(8,128)(2,1)S(1)}, u32[]{:S(2)}, u32[]{:S(2)}) collective-permute-start(bf16[192,512]{1,0:T(8,128)(2,1)} %get-tuple-element.11), channel_id=1, source_target_pairs={{0,8},{4,12},{8,0},{12,4},{16,24},{20,28},{24,16},{28,20},{1,9},{5... | collective-permute-start | bytes 589832 | tf_op jit(solution)/shard_map/ppermute | solution.py:18
  19.1 22.9 %collective-permute-start.13 = (bf16[192,512]{1,0:T(8,128)(2,1)}, bf16[192,512]{1,0:T(8,128)(2,1)}, u32[]{:S(2)}, u32[]{:S(2)}) collective-permute-start(bf16[192,512]{1,0:T(8,128)(2,1)} %get-tuple-element.10), channel_id=1, source_target_pairs={{0,12},{4,8},{8,4},{12,0},{16,28},{20,24},{24,20},{28,16},{1,13},{... | collective-permute-start | bytes 589832 | tf_op jit(solution)/shard_map/ppermute | solution.py:18
  19.8 18.4 %collective-permute-start.7 = (bf16[128,1536]{1,0:T(8,128)(2,1)S(1)}, bf16[128,1536]{1,0:T(8,128)(2,1)S(1)}, u32[]{:S(2)}, u32[]{:S(2)}) collective-permute-start(bf16[128,1536]{1,0:T(8,128)(2,1)S(1)} %bitcast.40), channel_id=1, source_target_pairs={{0,16},{4,20},{8,24},{12,28},{16,0},{20,4},{24,8},{28,12},{1,17},{... | collective-permute-start | bytes 1179656 | tf_op jit(solution)/shard_map/ppermute | solution.py:18
  22.9 19.5 %collective-permute-start = (bf16[192,512]{1,0:T(8,128)(2,1)}, bf16[192,512]{1,0:T(8,128)(2,1)S(1)}, u32[]{:S(2)}, u32[]{:S(2)}) collective-permute-start(bf16[192,512]{1,0:T(8,128)(2,1)} %get-tuple-element.16), channel_id=1, source_target_pairs={{0,4},{4,0},{8,12},{12,8},{16,20},{20,16},{24,28},{28,24},{1,5},{5... | collective-permute-start | bytes 589832 | tf_op jit(solution)/shard_map/ppermute | solution.py:18
  38.2 19.0 %collective-permute-start.4 = (bf16[128,1536]{1,0:T(8,128)(2,1)S(1)}, bf16[128,1536]{1,0:T(8,128)(2,1)S(1)}, u32[]{:S(2)}, u32[]{:S(2)}) collective-permute-start(bf16[128,1536]{1,0:T(8,128)(2,1)S(1)} %bitcast.41), channel_id=1, source_target_pairs={{0,2},{1,3},{2,0},{3,1},{4,6},{5,7},{6,4},{7,5},{8,10},{9,11},{10,... | collective-permute-start | bytes 1179656 | tf_op jit(solution)/shard_map/ppermute | solution.py:18
  41.1 16.1 %copy-start.1 = (bf16[128,1536]{1,0:T(8,128)(2,1)}, bf16[128,1536]{1,0:T(8,128)(2,1)S(1)}, u32[]{:S(2)}) copy-start(bf16[128,1536]{1,0:T(8,128)(2,1)S(1)} %shard_map.95.rest_4_) | copy-start | bytes 1179652
  41.1 16.6 %collective-permute-start.8 = (bf16[128,1536]{1,0:T(8,128)(2,1)S(1)}, bf16[128,1536]{1,0:T(8,128)(2,1)S(1)}, u32[]{:S(2)}, u32[]{:S(2)}) collective-permute-start(bf16[128,1536]{1,0:T(8,128)(2,1)S(1)} %shard_map.95.rest_4_), channel_id=1, source_target_pairs={{0,2},{1,3},{2,0},{3,1},{4,6},{5,7},{6,4},{7,5},{8,10},{9,11},{10,... | collective-permute-start | bytes 1179656 | tf_op jit(solution)/shard_map/ppermute | solution.py:18
  42.0 16.9 %collective-permute-start.5 = (bf16[128,1536]{1,0:T(8,128)(2,1)S(1)}, bf16[128,1536]{1,0:T(8,128)(2,1)S(1)}, u32[]{:S(2)}, u32[]{:S(2)}) collective-permute-start(bf16[128,1536]{1,0:T(8,128)(2,1)S(1)} %bitcast.42), channel_id=1, source_target_pairs={{0,1},{1,0},{2,3},{3,2},{4,5},{5,4},{6,7},{7,6},{8,9},{9,8},{10,11... | collective-permute-start | bytes 1179656 | tf_op jit(solution)/shard_map/ppermute | solution.py:18
  42.0 8.1 %collective-permute-start.1 = (bf16[192,512]{1,0:T(8,128)(2,1)}, bf16[192,512]{1,0:T(8,128)(2,1)S(1)}, u32[]{:S(2)}, u32[]{:S(2)}) collective-permute-start(bf16[192,512]{1,0:T(8,128)(2,1)} %get-tuple-element.15), channel_id=1, source_target_pairs={{0,8},{4,12},{8,0},{12,4},{16,24},{20,28},{24,16},{28,20},{1,9},{5... | collective-permute-start | bytes 589832 | tf_op jit(solution)/shard_map/ppermute | solution.py:18
  42.3 14.8 %collective-permute-start.2 = (bf16[192,512]{1,0:T(8,128)(2,1)S(1)}, bf16[192,512]{1,0:T(8,128)(2,1)S(1)}, u32[]{:S(2)}, u32[]{:S(2)}) collective-permute-start(bf16[192,512]{1,0:T(8,128)(2,1)S(1)} %get-tuple-element.14), channel_id=1, source_target_pairs={{0,12},{4,8},{8,4},{12,0},{16,28},{20,24},{24,20},{28,16},{1,13},{... | collective-permute-start | bytes 589832 | tf_op jit(solution)/shard_map/ppermute | solution.py:18
  47.0 11.8 %copy-start.3 = (bf16[192,1024]{1,0:T(8,128)(2,1)}, bf16[192,1024]{1,0:T(8,128)(2,1)S(1)}, u32[]{:S(2)}) copy-start(bf16[192,1024]{1,0:T(8,128)(2,1)S(1)} %shard_map.96.mine_ref) | copy-start | bytes 1179652
  50.0 29.7 %collective-permute-start.14 = (bf16[192,1024]{1,0:T(8,128)(2,1)S(1)}, bf16[192,1024]{1,0:T(8,128)(2,1)S(1)}, u32[]{:S(2)}, u32[]{:S(2)}) collective-permute-start(bf16[192,1024]{1,0:T(8,128)(2,1)S(1)} %shard_map.96.mine_ref), channel_id=1, source_target_pairs={{0,16},{4,20},{8,24},{12,28},{16,0},{20,4},{24,8},{28,12},{1,17},{... | collective-permute-start | bytes 1179656 | tf_op jit(solution)/shard_map/ppermute | solution.py:18
  57.2 22.6 %collective-permute-start.9 = (bf16[128,1536]{1,0:T(8,128)(2,1)S(1)}, bf16[128,1536]{1,0:T(8,128)(2,1)S(1)}, u32[]{:S(2)}, u32[]{:S(2)}) collective-permute-start(bf16[128,1536]{1,0:T(8,128)(2,1)S(1)} %shard_map.95.rest_4_), channel_id=1, source_target_pairs={{0,1},{1,0},{2,3},{3,2},{4,5},{5,4},{6,7},{7,6},{8,9},{9,8},{10,11... | collective-permute-start | bytes 1179656 | tf_op jit(solution)/shard_map/ppermute | solution.py:18
  57.2 1.7 %copy-start.7 = (bf16[128,1536]{1,0:T(8,128)(2,1)}, bf16[128,1536]{1,0:T(8,128)(2,1)S(1)}, u32[]{:S(2)}) copy-start(bf16[128,1536]{1,0:T(8,128)(2,1)S(1)} %collective-permute-done.4.rest_1_) | copy-start | bytes 1179652
  57.2 22.6 %collective-permute-start.6 = (bf16[128,1536]{1,0:T(8,128)(2,1)S(1)}, bf16[128,1536]{1,0:T(8,128)(2,1)S(1)}, u32[]{:S(2)}, u32[]{:S(2)}) collective-permute-start(bf16[128,1536]{1,0:T(8,128)(2,1)S(1)} %collective-permute-done.4.rest_1_), channel_id=1, source_target_pairs={{0,1},{1,0},{2,3},{3,2},{4,5},{5,4},{6,7},{7,6},{8,9},{9,8},{10,11... | collective-permute-start | bytes 1179656 | tf_op jit(solution)/shard_map/ppermute | solution.py:18
  57.7 1.2 %copy-start.8 = (bf16[128,1536]{1,0:T(8,128)(2,1)}, bf16[128,1536]{1,0:T(8,128)(2,1)S(1)}, u32[]{:S(2)}) copy-start(bf16[128,1536]{1,0:T(8,128)(2,1)S(1)} %collective-permute-done.8.rest_5_) | copy-start | bytes 1179652
  57.7 22.1 %collective-permute-start.10 = (bf16[128,1536]{1,0:T(8,128)(2,1)S(1)}, bf16[128,1536]{1,0:T(8,128)(2,1)S(1)}, u32[]{:S(2)}, u32[]{:S(2)}) collective-permute-start(bf16[128,1536]{1,0:T(8,128)(2,1)S(1)} %collective-permute-done.8.rest_5_), channel_id=1, source_target_pairs={{0,1},{1,0},{2,3},{3,2},{4,5},{5,4},{6,7},{7,6},{8,9},{9,8},{10,11... | collective-permute-start | bytes 1179656 | tf_op jit(solution)/shard_map/ppermute | solution.py:18
  57.8 1.2 %copy-start.16 = (f32[384]{0:T(512)S(1)}, f32[384]{0:T(512)}, u32[]{:S(2)}) copy-start(f32[384]{0:T(512)} %param.16) | copy-start | bytes 4612
  57.8 2.1 %copy-start.15 = (f32[2048]{0:T(1024)S(1)}, f32[2048]{0:T(1024)}, u32[]{:S(2)}) copy-start(f32[2048]{0:T(1024)} %param.15) | copy-start | bytes 24580
  57.8 2.1 %copy-start.5 = (s32[1,2,1536]{2,1,0:T(2,128)S(1)}, s32[1,2,1536]{2,1,0:T(2,128)}, u32[]{:S(2)}) copy-start(s32[1,2,1536]{2,1,0:T(2,128)} %param.14) | copy-start | bytes 36868
  58.9 7.0 %copy-start.2 = (bf16[192,1024]{1,0:T(8,128)(2,1)}, bf16[192,1024]{1,0:T(8,128)(2,1)S(1)}, u32[]{:S(2)}) copy-start(bf16[192,1024]{1,0:T(8,128)(2,1)S(1)} %shard_map.93.mine_ref) | copy-start | bytes 1179652
  58.9 7.0 %copy-start.9 = (bf16[128,1536]{1,0:T(8,128)(2,1)}, bf16[128,1536]{1,0:T(8,128)(2,1)S(1)}, u32[]{:S(2)}) copy-start(bf16[128,1536]{1,0:T(8,128)(2,1)S(1)} %collective-permute-done.5.rest_2_) | copy-start | bytes 1179652
  58.9 27.4 %collective-permute-start.3 = (bf16[192,1024]{1,0:T(8,128)(2,1)S(1)}, bf16[192,1024]{1,0:T(8,128)(2,1)S(1)}, u32[]{:S(2)}, u32[]{:S(2)}) collective-permute-start(bf16[192,1024]{1,0:T(8,128)(2,1)S(1)} %shard_map.93.mine_ref), channel_id=1, source_target_pairs={{0,16},{4,20},{8,24},{12,28},{16,0},{20,4},{24,8},{28,12},{1,17},{... | collective-permute-start | bytes 1179656 | tf_op jit(solution)/shard_map/ppermute | solution.py:18
  65.9 0.6 copy-start.4
  79.8 0.8 copy-start.14
  79.8 0.9 copy-start.10
  79.8 1.0 %copy-start.11 = (bf16[128,1536]{1,0:T(8,128)(2,1)}, bf16[128,1536]{1,0:T(8,128)(2,1)S(1)}, u32[]{:S(2)}) copy-start(bf16[128,1536]{1,0:T(8,128)(2,1)S(1)} %collective-permute-done.6.rest_3_) | copy-start | bytes 1179652
  79.8 1.1 %copy-start.12 = (bf16[128,1536]{1,0:T(8,128)(2,1)}, bf16[128,1536]{1,0:T(8,128)(2,1)S(1)}, u32[]{:S(2)}) copy-start(bf16[128,1536]{1,0:T(8,128)(2,1)S(1)} %collective-permute-done.10.rest_7_) | copy-start | bytes 1179652
  86.3 0.8 copy-start.13
